TPU v7x, 32 devices: a whole 2x2x4 slice. The times are simulated.
32 devices in a mesh: fsdp: 2 (over y), ctx: 4 (over x, core), tp: 4 (over z).
Axes of the slice: x: 2, y: 2, z: 4, core: 2. Of those that a mesh axis runs over, the one named last changes fastest.
Arguments:
- tokens: bfloat16 [4, 2048, 1024], P('fsdp', 'ctx'), may hold values from -6 to 6
- first_values: bfloat16 [4, 2048, 1024], P('fsdp', 'ctx', 'tp'), may hold values from -6 to 6
- norm1_gain: bfloat16 [1024], P('fsdp'), may hold values from 0.5 to 1.5
- norm2_gain: bfloat16 [1024], P('fsdp'), may hold values from 0.5 to 1.5
- w_query: bfloat16 [1024, 1024], P('fsdp', 'tp'), may hold values from -0.1875 to 0.1875
- w_key: bfloat16 [1024, 1024], P('fsdp', 'tp'), may hold values from -0.1875 to 0.1875
- w_value: bfloat16 [1024, 1024], P('fsdp', 'tp'), may hold values from -0.1875 to 0.1875
- w_out: bfloat16 [1024, 1024], P('tp', 'fsdp'), may hold values from -2 to 2
- w_gate: bfloat16 [1024, 2816], P('fsdp', 'tp'), may hold values from -0.1875 to 0.1875
- w_up: bfloat16 [1024, 2816], P('fsdp', 'tp'), may hold values from -0.1875 to 0.1875
- w_down: bfloat16 [2816, 1024], P('tp', 'fsdp'), may hold values from -0.109375 to 0.109375
- prefix: int32 [4], P('fsdp'), may hold values from 204 to 1024
- cotangent: bfloat16 [4, 2048, 1024], P('fsdp', 'ctx'), may hold values from -6 to 6
Outputs:
- block_out: bfloat16 [4, 2048, 1024], P('fsdp', 'ctx')
- token_grad: float32 [4, 2048, 1024], P('fsdp', 'ctx')
- first_values_grad: float32 [4, 2048, 1024], P('fsdp', 'ctx', 'tp')
- norm1_gain_grad: float32 [1024], P('fsdp')
- norm2_gain_grad: float32 [1024], P('fsdp')
- w_query_grad: float32 [1024, 1024], P('fsdp', 'tp')
- w_key_grad: float32 [1024, 1024], P('fsdp', 'tp')
- w_value_grad: float32 [1024, 1024], P('fsdp', 'tp')
- w_out_grad: float32 [1024, 1024], P('tp', 'fsdp')
- w_gate_grad: float32 [1024, 2816], P('fsdp', 'tp')
- w_up_grad: float32 [1024, 2816], P('fsdp', 'tp')
- w_down_grad: float32 [2816, 1024], P('tp', 'fsdp')
All inputs are finite; a program needn't handle non-finite values.
Results may differ from a plain program's by a relative error of at most 0.023.
Values may be sent and summed in bfloat16 or wider, within the bound.
A program may use at most 128 MiB of HBM per device.

v0:
```python
import functools

import jax
import jax.numpy as jnp
import numpy as np
from jax import lax
from jax.experimental import pallas as pl
from jax.experimental.pallas import tpu as pltpu
from jax.sharding import PartitionSpec as P

HEAD_DIM = 64
epsilon = 1e-06
rope_base = 10000.0
masked_score = -1e30
MESH = pl.DeviceIdType.MESH
bf16 = jnp.bfloat16
f32 = jnp.float32


def dot(a, b):
    return jnp.dot(a, b, preferred_element_type=f32)


def dot_nt(a, b):
    return lax.dot_general(a, b, (((1,), (1,)), ((), ())), preferred_element_type=f32)


def unit_norm(values):
    return values * lax.rsqrt(jnp.mean(values * values, axis=-1, keepdims=True) + epsilon)


def low_half(shape):
    return lax.rem(lax.broadcasted_iota(jnp.int32, shape, 1), HEAD_DIM) < HEAD_DIM // 2


class Sum:
    def __init__(self, place, part, inward, across, sems, done):
        self.pair = near(place)
        self.middle = 3 - place
        self.inner = (place == 1) | (place == 2)
        self.outer = (place == 0) | (place == 3)
        self.part, self.inward, self.across, self.done = part, inward, across, done
        self.send_one, self.recv_one, self.send_two, self.recv_two = sems

    def copy_in(self, i):
        return remote(
            self.part.at[i], self.inward.at[i], self.send_one.at[i], self.recv_one.at[i], {"tp": self.pair})

    def copy_across(self, i):
        return remote(
            self.part.at[i], self.across.at[i], self.send_two.at[i], self.recv_two.at[i], {"tp": self.middle})

    def copy_out(self, i):
        return remote(
            self.part.at[i], self.inward.at[i], self.send_one.at[i], self.recv_one.at[i], {"tp": self.pair})

    def fill(self, first, piece, values):
        chunk, size = self.part.shape[1], values.shape[1]
        for k in range(values.shape[0] // chunk):
            self.part[first + k, :, piece * size : (piece + 1) * size] = values[
                k * chunk : (k + 1) * chunk].astype(bf16)

    def offer(self, first, count):
        @pl.when(self.outer)
        def _():
            @pl.loop(0, count)
            def _(k):
                self.copy_in(first + k).start()

    def take_in(self, i):
        self.copy_in(i).wait_recv()
        self.part[i] = (self.part[i].astype(f32) + self.inward[i].astype(f32)).astype(bf16)
        self.copy_across(i).start()

    def finish(self, i):
        self.copy_across(i).wait()
        self.part[i] = (self.part[i].astype(f32) + self.across[i].astype(f32)).astype(bf16)
        self.copy_out(i).start()
        self.done(i)

    def steps(self, first, count):
        @pl.when(self.inner)
        def _():
            @pl.loop(first, first + count)
            def _(i):
                self.take_in(i)

                @pl.when(i > 0)
                def _():
                    self.finish(i - 1)

    def settled(self, first, count):
        @pl.when(self.outer)
        def _():
            @pl.loop(first, first + count)
            def _(i):
                self.copy_out(i).wait_recv()
                self.copy_in(i).wait_send()
                self.part[i] = self.inward[i]
                self.done(i)

    def close(self, count):
        @pl.when(self.inner)
        def _():
            self.finish(count - 1)

            @pl.loop(0, count)
            def _(i):
                self.copy_out(i).wait_send()


def near(place):
    return place + 1 - 2 * lax.rem(place, 2)


def greet(peers):
    barrier = pltpu.get_barrier_semaphore()
    for peer in peers:
        pl.semaphore_signal(barrier, inc=1, device_id=peer, device_id_type=MESH)
    pl.semaphore_wait(barrier, len(peers))


def block_place(ring, j):
    return jnp.where(
        j == 0, ring, jnp.where(j == 1, near(ring), jnp.where(j == 2, lax.rem(ring + 2, 4), 3 - ring)))


def line_peers(place):
    return [{"tp": near(place)}, {"tp": 3 - place}]


def ring_peers(ring):
    return [{"ctx": near(ring)}, {"ctx": lax.rem(ring + 2, 4)}]


def remote(source, target, send, recv, device):
    return pltpu.make_async_remote_copy(
        src_ref=source, dst_ref=target, send_sem=send, recv_sem=recv,
        device_id=device, device_id_type=MESH)


class Passing:
    def __init__(self, place, spot, sems, own=None):
        self.place, self.spot, self.own = place, spot, own
        self.send, self.recv = sems

    def move(self, piece, item, way, source=None):
        here = self.spot(piece, item)
        return remote(
            here if source is None else source, here, self.send.at[item, way, piece], self.recv.at[item, piece],
            {"tp": self.place + 1 - 2 * way})

    def begin(self, item):
        source = None if self.own is None else self.own(item)

        @pl.when(self.place < 3)
        def _():
            self.move(self.place, item, 0, source).start()

        @pl.when(self.place > 0)
        def _():
            self.move(self.place, item, 1, source).start()

    def step(self, item, distance):
        @pl.when(self.place >= distance)
        def _():
            piece = self.place - distance
            self.move(piece, item, 0).wait_recv()

            @pl.when(self.place < 3)
            def _():
                self.move(piece, item, 0).start()

        @pl.when(self.place + distance <= 3)
        def _():
            piece = self.place + distance
            self.move(piece, item, 1).wait_recv()

            @pl.when(self.place > 0)
            def _():
                self.move(piece, item, 1).start()

    def settle(self, items):
        for item in range(items):
            @pl.loop(0, 4)
            def _(piece, item=item):
                @pl.when((self.place < 3) & (piece <= self.place))
                def _():
                    self.move(piece, item, 0).wait_send()

                @pl.when((self.place > 0) & (piece >= self.place))
                def _():
                    self.move(piece, item, 1).wait_send()


def rows_at(start, size):
    return pl.ds(pl.multiple_of(start, size), size)


class Fold:
    def __init__(self, side, ring, grad, refs, sems, saved, ahead=None):
        self.ahead = ahead
        self.side, self.half = side, lax.rem(ring, 2)
        self.grad = grad
        self.one, self.two, self.three, self.final, self.wide = refs
        self.send, self.recv, self.save = sems
        self.mate, self.peer, self.other = (
            {"ctx": near(ring)}, {"ctx": lax.rem(ring + 2, 4)}, {"fsdp": 1 - side})
        self.saved = saved

    def copy(self, n):
        source, target, device = (
            (self.grad.at[1 - self.half], self.one, self.mate),
            (self.grad.at[self.half, 1 - self.side], self.two, self.other),
            (self.grad.at[self.half, self.side], self.three, self.peer),
            (self.final.at[self.half], self.final.at[self.half], self.mate),
        )[n]
        return remote(source, target, self.send.at[n], self.recv.at[n], device)

    def first(self):
        self.copy(0).start()

    def second(self):
        self.copy(0).wait_recv()
        for side in range(2):
            self.grad[self.half, side] = (
                self.grad[self.half, side].astype(f32) + self.one[side].astype(f32)).astype(bf16)
        self.copy(1).start()

    def third(self):
        self.copy(1).wait_recv()
        self.grad[self.half, self.side] = (
            self.grad[self.half, self.side].astype(f32) + self.two[...].astype(f32)).astype(bf16)
        self.copy(2).start()

    def fourth(self):
        self.copy(2).wait_recv()
        self.final[self.half] = (
            self.grad[self.half, self.side].astype(f32) + self.three[...].astype(f32)).astype(bf16)
        self.copy(3).start()

    def saving(self):
        return pltpu.make_async_copy(self.wide, self.saved, self.save)

    def last(self):
        self.copy(3).wait_recv()
        if self.ahead is not None:
            self.ahead.saving().wait()
        self.wide[...] = self.final[...].astype(f32)
        self.saving().start()

    def settle(self, saving=True):
        for n in range(4):
            self.copy(n).wait_send()
        if saving:
            self.saving().wait()


class Whole:
    def __init__(self, grad, sems, saved):
        self.copy = lambda: pltpu.make_async_copy(grad, saved, sems[2])

    def first(self):
        self.copy().start()

    def second(self):
        pass

    third = fourth = last = second

    def settle(self, saving=True):
        self.copy().wait()


def fold_shapes(shapes, split, shared=False):
    scratch = []
    for n, (r, c) in enumerate(shapes):
        scratch.append(pltpu.VMEM((2, 2, r, c), bf16))
        if split:
            scratch += [pltpu.VMEM((2, r, c), bf16), pltpu.VMEM((r, c), bf16), pltpu.VMEM((r, c), bf16),
                        pltpu.VMEM((2, r, c), bf16)]
            if n == 0 or not shared:
                scratch.append(pltpu.VMEM((2, r, c), f32))
    n = len(shapes)
    dma = pltpu.SemaphoreType.DMA
    scratch += [dma((n, 4)), dma((n, 4)), dma((n,))]
    outs = [
        jax.ShapeDtypeStruct((2, r, c), f32) if split else jax.ShapeDtypeStruct((2, 2, r, c), bf16)
        for r, c in shapes]
    return scratch, outs


def make_folds(split, side, ring, scratch, saved, shared=False):
    send, recv, save = scratch[-3:]
    folds, grads = [], []
    at = 0
    for n, target in enumerate(saved):
        sems = (send.at[n], recv.at[n], save.at[n])
        grads.append(scratch[at])
        if not split:
            folds.append(Whole(scratch[at], sems, target))
            at += 1
            continue
        own_wide = n == 0 or not shared
        refs = list(scratch[at + 1 : at + 5]) + [scratch[at + 5] if own_wide else scratch[5]]
        folds.append(Fold(side, ring, scratch[at], refs, sems, target, None if own_wide else folds[-1]))
        at += 6 if own_wide else 5
    return folds, grads


def turn(values, cosine, sine, sign=1.0):
    pieces = []
    half = HEAD_DIM // 2
    sine = sine * sign
    for at in range(0, values.shape[1], 128):
        piece = values[:, at : at + 128]
        swapped = jnp.where(
            low_half(piece.shape), pltpu.roll(piece, 128 - half, 1), pltpu.roll(piece, half, 1))
        pieces.append(piece * cosine + swapped * sine)
    return jnp.concatenate(pieces, axis=1)


def spread(target, values_t, start, rows):
    owner = lax.broadcasted_iota(jnp.int32, values_t.shape, 0) // HEAD_DIM
    for h in range(values_t.shape[0] // HEAD_DIM):
        target[h // 2, :, rows_at(h % 2 * rows + start, values_t.shape[1])] = jnp.where(
            owner == h, values_t, 0.0).astype(bf16)


def gain_row(gains, which):
    return jnp.concatenate([gains[0, which : which + 1, :], gains[1, which : which + 1, :]], axis=1)


def front_kernel(split, *refs):
    place, ring, side = lax.axis_index("tp"), lax.axis_index("ctx"), lax.axis_index("fsdp")
    (tok, fv, cot_hbm, gain_in, wq_in, wk_in, wv_in, wo_in, wg_in, wu_in, wd_in), refs = refs[:11], refs[11:]
    (frequency, prefix, sum_hbm, late_hbm, q_out, kv_hbm, attn_hbm, ctx_hbm, lse_out, gains, cosine, sine), refs = (
        refs[:12], refs[12:])
    saved, refs = refs[:3], refs[3:]
    if split:
        (wq_hbm, wk_hbm, wv_hbm, wo_hbm), refs = refs[:4], refs[4:]
        (wq, wk, wv, w_send, w_recv, w_save, g_sems, o_send, o_recv), refs = refs[:9], refs[9:]
    else:
        wq, wk, wv = wq_in, wk_in, wv_in
    (normed_s, kv, qtm, vt, acct, maxes, totals, part, inward, across,
     kv_send, kv_recv, kv_save, send_one, recv_one, send_two, recv_two, save,
     wg, wu, wd, loads, cot, inner_t, gg_t, ug_t, late, late_save, wo_all, ctx_all, attn,
     p_send, p_recv, c_send, c_recv, c_save, a_save), refs = refs[:37], refs[37:]
    (fold_d, fold_g, fold_u), grads = make_folds(split, side, ring, refs, saved, True)
    seqs, rows, width = q_out.shape
    heads = width // HEAD_DIM
    tile = 256
    chunk, dim = part.shape[1:]
    per_seq = rows // chunk
    per_tile = tile // chunk
    middle = dim // 2
    units = wg_in.shape[-2]
    mate, peer = ring_peers(ring)
    half = lax.rem(ring, 2)
    for full in (wg, wu, wd):
        for piece in range(2):
            full[piece, units:] = jnp.zeros((full.shape[1] - units, full.shape[2]), bf16)
    own_loads = [pltpu.make_async_copy(cot_hbm, cot, loads.at[6])]
    for n, (source, full) in enumerate(((wg_in, wg), (wu_in, wu), (wd_in, wd))):
        if split:
            own_loads.append(pltpu.make_async_copy(source, full.at[side, 0:units], loads.at[n]))
        else:
            for piece in range(2):
                own_loads.append(pltpu.make_async_copy(
                    source.at[piece], full.at[piece, 0:units], loads.at[2 * n + piece]))
    greet(line_peers(place) + ring_peers(ring) + ([{"fsdp": 1 - side}] if split else []))

    if split:
        other = {"fsdp": 1 - side}
        gains[side, 0:2, :] = gain_in[...]
        move_gains = remote(gains.at[side], gains.at[side], g_sems.at[0], g_sems.at[1], other)
        move_gains.start()

        def spot(full, owner, part_at, size):
            if full is wo_all:
                return full.at[place, owner, rows_at(part_at * size, size)]
            if full.shape[0] == 2:
                return full.at[owner, rows_at(part_at * size, size)]
            return full.at[rows_at((2 * owner + part_at) * size, size)]

        table = (
            (wk_in, wk, spot), (wv_in, wv, spot), (wq_in, wq, spot), (wo_in, wo_all, spot),
            (wg_in, wg, spot), (wu_in, wu, spot), (wd_in, wd, spot))

        def cross(n):
            own, full, where = table[n]
            size = own.shape[0] // 2
            return remote(own.at[rows_at(half * size, size)], where(full, side, half, size),
                          w_send.at[n, 0], w_recv.at[n, 0], other)

        def onto_mate(n):
            own, full, where = table[n]
            here = where(full, 1 - side, half, own.shape[0] // 2)
            return remote(here, here, w_send.at[n, 1], w_recv.at[n, 1], mate)

        def hand_on(n):
            cross(n).wait_recv()
            onto_mate(n).start()

        saves = tuple(
            pltpu.make_async_copy(full, target, w_save.at[n])
            for n, (full, target) in enumerate(((wk, wk_hbm), (wv, wv_hbm), (wq, wq_hbm), (wo_all.at[place], wo_hbm))))
        for n in (0, 1, 3):
            cross(n).start()
        for own, full, _ in table[:3]:
            full[rows_at(side * own.shape[0], own.shape[0]), :] = own[...]
        wo_all[place, side] = wo_in[...]
        part_o = wo_in.shape[0] // 2
        item_side = lambda item: side if item == 0 else 1 - side
        pass_o = Passing(
            place, lambda piece, item: wo_all.at[piece, item_side(item), rows_at(half * part_o, part_o)],
            (p_send, p_recv),
            lambda item: wo_in.at[rows_at(half * part_o, part_o)] if item == 0 else None)
        pass_o.begin(0)

        def share_o(n):
            here = wo_all.at[lax.rem(place + n + 1, 4), :, rows_at(half * part_o, part_o)]
            return remote(here, here, o_send.at[n], o_recv.at[n], mate)
        remote(gains.at[side], gains.at[side], g_sems.at[0], g_sems.at[1], other).wait()
    else:
        size = gains.shape[2]
        for piece in range(2):
            gains[piece, 0:2, :] = gain_in[:, piece * size : (piece + 1) * size]
        wo_all[place] = wo_in[...]
        pass_o = Passing(place, lambda piece, item: wo_all.at[piece, item], (p_send, p_recv))
        pass_o.begin(0)
        pass_o.begin(1)

    for load in own_loads:
        load.start()

    def pass_block(s, source, target, device, slot):
        return remote(kv.at[s, source], kv.at[s, target], kv_send.at[s, slot], kv_recv.at[s, target], device)

    to_mate = lambda s: pass_block(s, 0, 1, mate, 0)
    to_peer = lambda s: pass_block(s, 0, 2, peer, 1)
    onward = lambda s: pass_block(s, 2, 3, mate, 2)
    gain_one = gain_row(gains, 0)
    position = (ring * rows + lax.broadcasted_iota(jnp.int32, cosine.shape, 0)).astype(f32)
    angles = position * frequency[0:1, :]
    cosine[...] = jnp.cos(angles)
    sine[...] = jnp.sin(angles) * jnp.where(low_half(cosine.shape), -1.0, 1.0)

    per_seq_tiles = rows // tile
    tiles = seqs * per_seq_tiles

    def tile_at(t):
        return t // per_seq_tiles, rows_at(lax.rem(t, per_seq_tiles) * tile, tile)

    @pl.loop(0, tiles)
    def _(t):
        s, at = tile_at(t)
        normed_s[s, at, :] = (unit_norm(tok[s, at, :].astype(f32)) * gain_one).astype(bf16)

    if split:
        hand_on(0)
        hand_on(1)
        cross(2).start()
        pass_o.step(0, 1)
        onto_mate(0).wait_recv()
        onto_mate(1).wait_recv()

    @pl.loop(0, tiles)
    def _(t):
        s, at = tile_at(t)
        normed = normed_s[s, at, :]
        k = dot(normed, wk[...])
        kv[s, 0, 0, at, :] = turn(k, cosine[at, :], sine[at, :]).astype(bf16)
        v = dot(normed, wv[...])
        kv[s, 0, 1, at, :] = (0.5 * v + 0.5 * fv[s, at, :].astype(f32)).astype(bf16)

        @pl.when(lax.rem(t, per_seq_tiles) == per_seq_tiles - 1)
        def _():
            to_peer(s).start()
            to_mate(s).start()

    if split:
        hand_on(3)
        pass_o.step(0, 2)
        pass_o.begin(1)
        hand_on(2)
        for n in range(4, 7):
            cross(n).start()
        onto_mate(2).wait_recv()

    @pl.loop(0, tiles)
    def _(t):
        s, at = tile_at(t)
        q = dot(normed_s[s, at, :], wq[...])
        q = turn(q, cosine[at, :], sine[at, :]) * HEAD_DIM ** (-0.5)
        q_out[s, at, :] = q.astype(bf16)
        spread(qtm.at[s], jnp.transpose(q), lax.rem(t, per_seq_tiles) * tile, rows)

    if not split:
        pass_o.step(0, 1)
        pass_o.step(0, 2)
    pass_o.step(0, 3)
    pass_o.step(1, 1)

    def saving(i):
        return pltpu.make_async_copy(part.at[i], sum_hbm.at[i], save.at[i])

    sums = Sum(
        place, part, inward, across, (send_one, recv_one, send_two, recv_two), lambda i: saving(i).start())
    passing = Passing(place, lambda piece, item: ctx_all.at[piece, item], (c_send, c_recv))

    def saving_context(s):
        mine = pl.ds(s * per_seq_tiles, per_seq_tiles)
        return pltpu.make_async_copy(ctx_all.at[place, mine], ctx_hbm.at[mine], c_save.at[s])

    def saving_kv(s):
        return pltpu.make_async_copy(kv.at[s], kv_hbm.at[s], kv_save.at[s])

    @pl.loop(0, seqs)
    def _(s):
        maxes[...] = jnp.full_like(maxes, masked_score)
        totals[...] = jnp.zeros_like(totals)
        acct[...] = jnp.zeros_like(acct)

        @pl.loop(0, 4)
        def _(j):
            @pl.when(j == 1)
            def _():
                to_mate(s).wait_recv()

            @pl.when(j == 2)
            def _():
                to_peer(s).wait_recv()
                onward(s).start()

            @pl.when(j == 3)
            def _():
                onward(s).wait_recv()

            vt[...] = jnp.transpose(kv[s, j, 1])
            key_pos = block_place(ring, j) * rows + lax.broadcasted_iota(jnp.int32, (rows, 1), 0)
            query_pos = ring * rows + lax.rem(lax.broadcasted_iota(jnp.int32, (1, 2 * rows), 1), rows)
            seen = key_pos < jnp.maximum(query_pos + 1, prefix[s])

            @pl.loop(0, heads // 2)
            def _(h):
                scores = jnp.where(seen, dot(kv[s, j, 0], qtm[s, h]), masked_score)
                old = maxes[h]
                new = jnp.maximum(old, jnp.max(scores, axis=0, keepdims=True))
                weights = jnp.exp(scores - new)
                fade = jnp.exp(old - new)
                maxes[h] = new
                totals[h] = totals[h] * fade + jnp.sum(weights, axis=0, keepdims=True)
                low = weights.astype(bf16)
                for n in range(2):
                    of_head = rows_at((2 * h + n) * HEAD_DIM, HEAD_DIM)
                    lanes = slice(n * rows, (n + 1) * rows)
                    acct[of_head, :] = acct[of_head, :] * fade[:, lanes] + dot(vt[of_head, :], low[:, lanes])
                at_step = j * (heads // 2) + h

                @pl.when((s > 0) & (at_step < 3 * per_seq_tiles))
                def _():
                    passing.step(
                        (s - 1) * per_seq_tiles + lax.rem(at_step, per_seq_tiles), 1 + at_step // per_seq_tiles)

        for h in range(heads):
            if h % 2 == 0:
                lse_out[s, h // 2 : h // 2 + 1, :] = maxes[h // 2] + jnp.log(totals[h // 2])
            of_head = slice(h * HEAD_DIM, (h + 1) * HEAD_DIM)
            acct[of_head, :] = acct[of_head, :] / totals[h // 2][:, h % 2 * rows : (h % 2 + 1) * rows]
        for t in range(per_seq_tiles):
            ctx_all[place, s * per_seq_tiles + t] = jnp.transpose(acct[:, t * tile : (t + 1) * tile]).astype(bf16)
        for t in range(per_seq_tiles):
            passing.begin(s * per_seq_tiles + t)
        saving_context(s).start()
        saving_kv(s).start()

        @pl.when(s == 0)
        def _():
            pass_o.step(1, 2)
            if split:
                onto_mate(3).wait_recv()
                for copy in saves:
                    copy.start()
                hand_on(4)
                hand_on(5)

    if split:
        hand_on(6)
    pass_o.step(1, 3)
    if split:
        for n in range(3):
            share_o(n).start()
        for n in range(3):
            share_o(n).wait_recv()
    if split:
        for n in range(4, 7):
            onto_mate(n).wait_recv()
    for load in own_loads:
        load.wait()
    lines = seqs * per_seq
    early = lines
    count = part.shape[0]
    gain_two = gain_row(gains, 1)

    def saving_attn(t):
        mine = pl.ds(t * per_tile, per_tile)
        return pltpu.make_async_copy(attn.at[mine], attn_hbm.at[mine], a_save.at[t])

    def across_both(left, full):
        return dot_nt(left[:, :middle], full[0]) + dot_nt(left[:, middle:], full[1])

    def saving_late(t):
        mine = pl.ds((t - 1) * per_tile, per_tile)
        return pltpu.make_async_copy(late.at[mine], late_hbm.at[mine], late_save.at[t - 1])

    @pl.loop(0, tiles)
    def _(t):
        s, at = tile_at(t)
        flat = rows_at(t * tile, tile)
        mine = t * per_tile

        def tick(n):
            at_step = 3 * t + n

            @pl.when(t < per_seq_tiles)
            def _():
                passing.step(
                    (seqs - 1) * per_seq_tiles + lax.rem(at_step, per_seq_tiles), 1 + at_step // per_seq_tiles)

            @pl.when((t >= per_seq_tiles) & (n > 0))
            def _():
                sums.steps(2 * (t - per_seq_tiles) + n - 1, 1)

        context = jnp.concatenate([ctx_all[p, t] for p in range(4)], axis=1)
        attended = [
            dot(context, jnp.concatenate([wo_all[p, piece] for p in range(4)], axis=0)) for piece in range(2)]
        for piece in range(2):
            for k in range(per_tile):
                attn[mine + k, :, piece * middle : (piece + 1) * middle] = attended[piece][
                    k * chunk : (k + 1) * chunk].astype(bf16)
        saving_attn(t).start()
        hidden = tok[s, at, :].astype(f32) + jnp.concatenate(attended, axis=1)
        normed = (unit_norm(hidden) * gain_two).astype(bf16)
        normed_s[s, at, :] = normed
        gate = across_both(normed, wg)
        up = across_both(normed, wu)
        sigmoid = jax.nn.sigmoid(gate)
        swish = gate * sigmoid
        inner = (swish * up).astype(bf16)
        inner_t[:, flat] = jnp.transpose(inner)
        inner_grad = across_both(cot[s, at, :], wd)
        gate_grad = (inner_grad * up * sigmoid * (1.0 + gate * (1.0 - sigmoid))).astype(bf16)
        up_grad = (inner_grad * swish).astype(bf16)
        tick(0)
        for piece in range(2):
            sums.fill(mine, piece, dot(gate_grad, wg[piece]) + dot(up_grad, wu[piece]))
        sums.offer(mine, per_tile)
        tick(1)
        feeds = [dot(inner, wd[piece]) for piece in range(2)]

        @pl.when(t == 0)
        def _():
            for piece in range(2):
                sums.fill(early, piece, feeds[piece])

        @pl.when(t > 0)
        def _():
            for piece in range(2):
                for k in range(per_tile):
                    late[mine - per_tile + k, :, piece * middle : (piece + 1) * middle] = feeds[piece][
                        k * chunk : (k + 1) * chunk].astype(bf16)
            saving_late(t).start()

        gg_t[:, flat] = jnp.transpose(gate_grad)
        ug_t[:, flat] = jnp.transpose(up_grad)
        tick(2)

    sums.offer(early, count - early)
    deep = units // 2

    def weight_grad(n, left_t, right):
        for h in range(2):
            for y in range(2):
                total = jnp.zeros((deep, middle), f32)
                for s in range(seqs):
                    total = total + dot(
                        left_t[h * deep : (h + 1) * deep, s * rows : (s + 1) * rows],
                        right[s, :, y * middle : (y + 1) * middle])
                grads[n][h, y] = total.astype(bf16)

    begun = 2 * (tiles - per_seq_tiles)
    weight_grad(0, inner_t, cot)
    fold_d.first()
    sums.steps(begun, 1)
    weight_grad(1, gg_t, normed_s)
    fold_g.first()
    fold_d.second()
    sums.steps(begun + 1, 1)
    weight_grad(2, ug_t, normed_s)
    fold_u.first()
    fold_g.second()
    sums.steps(begun + 2, 1)
    fold_u.second()
    sums.steps(begun + 3, 2)
    fold_d.third()
    sums.steps(begun + 5, 3)
    fold_g.third()
    fold_d.fourth()
    sums.steps(begun + 8, 3)
    fold_u.third()
    fold_g.fourth()
    fold_d.last()
    sums.steps(begun + 11, 3)
    fold_u.fourth()
    fold_g.last()
    sums.steps(begun + 14, count - begun - 14)
    fold_u.last()
    sums.settled(0, count)
    sums.close(count)
    for fold in (fold_d, fold_g):
        fold.settle(False)
    fold_u.settle()
    for t in range(1, tiles):
        saving_late(t).wait()
    for s in range(seqs):
        to_mate(s).wait_send()
        to_peer(s).wait_send()
        onward(s).wait_send()
        saving_kv(s).wait()
        saving_context(s).wait()
    for t in range(tiles):
        saving_attn(t).wait()
    pass_o.settle(2)
    passing.settle(tiles)

    @pl.loop(0, count)
    def _(i):
        saving(i).wait()

    if split:
        for n in range(7):
            cross(n).wait_send()
            onto_mate(n).wait_send()
        for n in range(3):
            share_o(n).wait_send()
        for copy in saves:
            copy.wait()


def limits(ident, megabytes=60):
    return pltpu.CompilerParams(
        collective_id=ident, has_side_effects=True, vmem_limit_bytes=megabytes * 1024 * 1024)


def front(split, tok, fv, cot, gains, square, wide, frequency, prefix):
    seqs, rows, dim = tok.shape
    width, units = square[0].shape[1], wide[0].shape[-2]
    heads = width // HEAD_DIM
    chunk, tile = 64, 256
    tokens = seqs * rows
    count = tokens // chunk + tile // chunk
    after = (tokens - tile) // chunk
    padded = -(-units // 256) * 256
    vmem = pl.BlockSpec(memory_space=pltpu.VMEM)
    anyw = pl.BlockSpec(memory_space=pl.ANY)
    dma = pltpu.SemaphoreType.DMA
    lines = pltpu.VMEM((count, chunk, dim), bf16)
    shape = jax.ShapeDtypeStruct
    full = [(dim, width)] * 3 + [(2, width, dim // 2)]
    fold_scratch, fold_outs = fold_shapes([(units // 2, dim // 2)] * 3, split, True)
    outs = [
        shape((count, chunk, dim), bf16), shape((after, chunk, dim), bf16), shape((seqs, rows, width), bf16),
        shape((seqs, 4, 2, rows, width), bf16), shape((tokens // chunk, chunk, dim), bf16),
        shape((tokens // tile, tile, width), bf16),
        shape((seqs, heads // 2, 2 * rows), f32), shape((2, 8, dim // 2), f32),
        shape((rows, 128), f32), shape((rows, 128), f32)] + fold_outs
    out_specs = [anyw, anyw, vmem, anyw, anyw, anyw, vmem, vmem, vmem, vmem] + [anyw] * 3
    scratch = []
    if split:
        outs += [shape(size, bf16) for size in full]
        out_specs += [anyw] * 4
        scratch = [pltpu.VMEM(size, bf16) for size in full[:3]] + [
            dma((7, 2)), dma((7, 2)), dma((4,)), dma((2,)), dma((3,)), dma((3,))]
    scratch += [
        pltpu.VMEM((seqs, rows, dim), bf16),
        pltpu.VMEM((seqs, 4, 2, rows, width), bf16),
        pltpu.VMEM((seqs, heads // 2, width, 2 * rows), bf16),
        pltpu.VMEM((width, rows), bf16),
        pltpu.VMEM((width, rows), f32),
        pltpu.VMEM((heads // 2, 1, 2 * rows), f32),
        pltpu.VMEM((heads // 2, 1, 2 * rows), f32),
        lines, lines, lines,
        dma((seqs, 3)), dma((seqs, 4)), dma((seqs,)),
        dma((count,)), dma((count,)), dma((count,)), dma((count,)), dma((count,)),
        pltpu.VMEM((2, padded, dim // 2), bf16),
        pltpu.VMEM((2, padded, dim // 2), bf16),
        pltpu.VMEM((2, padded, dim // 2), bf16),
        dma((7,)),
        pltpu.VMEM((seqs, rows, dim), bf16),
        pltpu.VMEM((padded, tokens), bf16),
        pltpu.VMEM((padded, tokens), bf16),
        pltpu.VMEM((padded, tokens), bf16),
        pltpu.VMEM((after, chunk, dim), bf16),
        dma((tokens // tile,)),
        pltpu.VMEM((4, 2, width, dim // 2), bf16),
        pltpu.VMEM((4, tokens // tile, tile, width), bf16),
        pltpu.VMEM((tokens // chunk, chunk, dim), bf16),
        dma((2, 2, 4)), dma((2, 4)), dma((tokens // tile, 2, 4)), dma((tokens // tile, 4)),
        dma((seqs,)), dma((tokens // tile,)),
    ] + fold_scratch
    return pl.pallas_call(
        functools.partial(front_kernel, split),
        name="front",
        out_shape=outs,
        in_specs=[vmem] * 2 + [anyw] + [vmem] * 5 + [anyw] * 3 + [vmem, pl.BlockSpec(memory_space=pltpu.SMEM)],
        out_specs=out_specs,
        scratch_shapes=scratch,
        compiler_params=limits(0, 63),
        cost_estimate=pl.CostEstimate(flops=22 * 10**9, bytes_accessed=2 * 10**7, transcendentals=10**7),
    )(tok, fv, cot, gains, *square, *wide, frequency, prefix)


def back_kernel(split, *refs):
    place, ring, side = lax.axis_index("tp"), lax.axis_index("ctx"), lax.axis_index("fsdp")
    loaded, refs = refs[:12], refs[12:]
    (gain_in, lse, cosine, sine, prefix, block_hbm, token_hbm, fv_out, gain_out), saved, refs = (
        refs[:9], refs[9:13], refs[13:])
    (tok, cot, wq, wk, wv, wo, q, kv, ctx, attn, mixed, early), refs = refs[:12], refs[12:]
    (hid, branch, qtm, qm, otm, om, kt, delta, dqt, dk, dv, give, take, proj, normed_t,
     part, inward, across, gain_part, gain_all,
     kv_send, kv_recv, send_one, recv_one, send_two, recv_two, save, gain_send, gain_recv, loads), refs = (
        refs[:30], refs[30:])
    (fold_o, fold_k, fold_v, fold_q), (dwo, dwk, dwv, dwq) = make_folds(split, side, ring, refs, saved)
    late_hbm, sum_hbm, attn_hbm, tok_hbm, cot_hbm, wq_hbm, wk_hbm, wv_hbm, wo_hbm, q_hbm, kv_hbm, ctx_hbm = loaded
    seqs, rows, dim = tok.shape
    width = wq.shape[1]
    heads = width // HEAD_DIM
    chunk = part.shape[1]
    per_seq = rows // chunk
    tile = 256
    per_tile = tile // chunk
    middle = dim // 2
    lines = seqs * per_seq
    count = 2 * lines - per_tile
    head_start, rest = per_seq, per_seq - per_tile
    rest_start = head_start + per_seq
    own_start = (head_start, rest_start + rest)
    mate, peer = ring_peers(ring)
    others = [(dy, dc) for dy in range(2) for dc in range(4) if dy or dc]
    group = [{"fsdp": lax.rem(side + dy, 2), "ctx": lax.rem(ring + dc, 4)} for dy, dc in others]

    copies = {}

    def load(name, source, target):
        copies[name] = pltpu.make_async_copy(source, target, loads.at[len(copies)])
        copies[name].start()

    def ready(*names):
        for name in names:
            copies[name].wait()

    load("late", late_hbm.at[0:head_start], part.at[0:head_start])
    for s in range(seqs):
        mine = slice(s * per_seq, (s + 1) * per_seq)
        load(f"tok{s}", tok_hbm.at[s], tok.at[s])
        load(f"attn{s}", attn_hbm.at[mine], attn.at[mine])
        load(f"cot{s}", cot_hbm.at[s], cot.at[s])
        load(f"mixed{s}", sum_hbm.at[mine], mixed.at[mine])
        if s == 0:
            load("wo", wo_hbm, wo)
        load(f"q{s}", q_hbm.at[s], q.at[s])
        load(f"ctx{s}", ctx_hbm.at[s], ctx.at[s])
        load(f"kv{s}", kv_hbm.at[s], kv.at[s])
    load("rest", late_hbm.at[head_start : head_start + rest], part.at[rest_start : rest_start + rest])
    load("early", sum_hbm.at[lines : lines + per_tile], early)
    load("wq", wq_hbm, wq)
    load("wk", wk_hbm, wk)
    load("wv", wv_hbm, wv)
    greet(line_peers(place) + (group if split else ring_peers(ring)))
    gain_one, gain_two = gain_row(gain_in, 0), gain_row(gain_in, 1)
    gain_part[...] = jnp.zeros_like(gain_part)

    def chunk_at(n):
        return n // per_seq, rows_at(lax.rem(n, per_seq) * chunk, chunk)

    def saving_block(i, n):
        s, own = chunk_at(n)
        return pltpu.make_async_copy(across.at[i], block_hbm.at[s, own], save.at[i])

    def saving_early(n):
        return pltpu.make_async_copy(early.at[n], block_hbm.at[0, n * chunk : (n + 1) * chunk], save.at[count + n])

    def saving_token(i, n):
        s, own = chunk_at(n)
        return pltpu.make_async_copy(hid.at[s, own], token_hbm.at[s, own], save.at[i])

    def add_gain(which, value):
        for piece in range(2):
            gain_part[piece, which : which + 1, :] += value[:, piece * middle : (piece + 1) * middle]

    is_block = lambda i: (i < head_start) | ((i >= rest_start) & (i < own_start[1]))
    block_of = lambda i: per_tile + jnp.where(i < head_start, i, i - per_seq)
    token_of = lambda i: jnp.where(i < rest_start, i - head_start, i - own_start[1] + per_seq)

    def done(i):
        @pl.when(is_block(i))
        def _():
            n = block_of(i)
            s, own = chunk_at(n)
            across[i] = (
                tok[s, own, :].astype(f32) + attn[n].astype(f32) + part[i].astype(f32)).astype(bf16)
            saving_block(i, n).start()

        @pl.when(jnp.logical_not(is_block(i)))
        def _():
            n = token_of(i)
            s, own = chunk_at(n)
            values, upstream = tok[s, own, :].astype(f32), part[i].astype(f32)
            factor = lax.rsqrt(jnp.mean(values * values, axis=-1, keepdims=True) + epsilon)
            scaled = upstream * gain_one
            add_gain(0, jnp.sum(upstream * values * factor, axis=0, keepdims=True))
            hid[s, own, :] += factor * scaled - values * factor**3 * jnp.mean(
                scaled * values, axis=-1, keepdims=True)
            saving_token(i, n).start()

    sums = Sum(place, part, inward, across, (send_one, recv_one, send_two, recv_two), done)

    def move(s, source, target, device):
        return remote(give.at[source], take.at[s, target], kv_send.at[source], kv_recv.at[s, target], device)

    far_to_mate = lambda s: move(s, 2, 0, mate)
    peer_back = lambda s: move(s, 1, 1, peer)
    near_to_mate = lambda s: move(s, 0, 2, mate)
    ready("late")
    sums.offer(0, head_start)

    def hidden_stage(s):
        @pl.loop(0, rows // tile)
        def _(t):
            at = rows_at(t * tile, tile)
            first = s * per_seq + t * per_tile
            join = lambda ref: jnp.concatenate([ref[first + k] for k in range(per_tile)], axis=0).astype(f32)
            token = tok[s, at, :].astype(f32)
            values = token + join(attn)
            upstream = join(mixed)
            factor = lax.rsqrt(jnp.mean(values * values, axis=-1, keepdims=True) + epsilon)
            scaled = upstream * gain_two
            add_gain(1, jnp.sum(upstream * values * factor, axis=0, keepdims=True))
            hid_now = cot[s, at, :].astype(f32) + factor * scaled - values * factor**3 * jnp.mean(
                scaled * values, axis=-1, keepdims=True)
            hid[s, at, :] = hid_now
            low = hid_now.astype(bf16)
            branch[s, at, :] = low
            left, right = low[:, :middle], low[:, middle:]
            grad = dot_nt(left, wo[0]) + dot_nt(right, wo[1])
            lane_owner = lax.broadcasted_iota(jnp.int32, grad.shape, 1) // HEAD_DIM
            q_now = q[s, at, :].astype(f32)
            grad_t = jnp.transpose(grad)
            q_t = jnp.transpose(q_now)
            product = jnp.transpose(grad.astype(bf16).astype(f32) * ctx[s, at, :].astype(f32))
            for h in range(heads):
                low_rows = rows_at(h % 2 * rows + t * tile, tile)
                om[h // 2, low_rows, :] = jnp.where(lane_owner == h, grad, 0.0).astype(bf16)
                qm[h // 2, low_rows, :] = jnp.where(lane_owner == h, q_now, 0.0).astype(bf16)
                delta[h // 2, :, low_rows] = jnp.sum(
                    product[h * HEAD_DIM : (h + 1) * HEAD_DIM], axis=0, keepdims=True)
            spread(otm, grad_t, t * tile, rows)
            spread(qtm, q_t, t * tile, rows)
            normed = (unit_norm(token) * gain_one).astype(bf16)
            normed_t[:, rows_at(s * rows + t * tile, tile)] = jnp.transpose(normed)

    def back_block(s, j):
        kt[...] = jnp.transpose(kv[s, j, 0])
        key_pos = block_place(ring, j) * rows + lax.broadcasted_iota(jnp.int32, (rows, 1), 0)
        query_pos = ring * rows + lax.rem(lax.broadcasted_iota(jnp.int32, (1, 2 * rows), 1), rows)
        seen = key_pos < jnp.maximum(query_pos + 1, prefix[s])
        dk[...] = jnp.zeros_like(dk)
        dv[...] = jnp.zeros_like(dv)

        @pl.loop(0, heads // 2)
        def _(h):
            scores = dot(kv[s, j, 0], qtm[h])
            probs = jnp.where(seen, jnp.exp(scores - lse[s, pl.ds(h, 1), :]), 0.0)
            dprobs = dot(kv[s, j, 1], otm[h])
            dv[...] += dot(probs.astype(bf16), om[h])
            dscores = (probs * (dprobs - delta[h])).astype(bf16)
            dk[...] += dot(dscores, qm[h])
            for n in range(2):
                of_head = rows_at((2 * h + n) * HEAD_DIM, HEAD_DIM)
                dqt[of_head, :] += dot(kt[of_head, :], dscores[:, n * rows : (n + 1) * rows])

    def finalize(s):
        near_to_mate(s).wait_recv()
        peer_back(s).wait_recv()
        @pl.loop(0, rows // tile)
        def _(t):
            at = rows_at(t * tile, tile)
            flat = rows_at(s * rows + t * tile, tile)
            co, si = cosine[at, :], sine[at, :]
            grad_v = 0.5 * (dv[at, :] + take[s, 2, 1, at, :].astype(f32) + take[s, 1, 1, at, :].astype(f32))
            grad_k = dk[at, :] + take[s, 2, 0, at, :].astype(f32) + take[s, 1, 0, at, :].astype(f32)
            grad_q = jnp.transpose(dqt[:, at]) * HEAD_DIM ** (-0.5)
            proj[0, flat, :] = turn(grad_q, co, si, -1.0).astype(bf16)
            proj[1, flat, :] = turn(grad_k, co, si, -1.0).astype(bf16)
            proj[2, flat, :] = grad_v.astype(bf16)
            fv_out[s, at, :] = grad_v
            i = jnp.where(s == 0, own_start[0], own_start[1]) + t * per_tile
            for piece in range(2):
                cut = slice(piece * middle, (piece + 1) * middle)
                sums.fill(i, piece, dot_nt(proj[0, flat, :], wq[cut, :]) + dot_nt(
                    proj[1, flat, :], wk[cut, :]) + dot_nt(proj[2, flat, :], wv[cut, :]))
            sums.offer(i, per_tile)

        @pl.when(s == 0)
        def _():
            sums.offer(rest_start, rest)

    ready("wo")

    def at_phase(phase, wanted, names):
        @pl.when(phase == wanted)
        def _():
            ready(*names)

    @pl.loop(0, seqs + 1)
    def _(phase):
        s = jnp.maximum(phase - 1, 0)
        follows = phase > 1

        @pl.when(phase > 0)
        def _():
            for wanted in range(seqs):
                at_phase(phase, wanted + 1, [f"kv{wanted}"])
            dqt[...] = jnp.zeros_like(dqt)

            @pl.loop(0, 4)
            def _(n):
                back_block(s, 3 - n)

                @pl.when(n == 0)
                def _():
                    @pl.when(follows)
                    def _():
                        far_to_mate(s - 1).wait_send()
                        fold_o.second()

                    give[2, 0] = dk[...].astype(bf16)
                    give[2, 1] = dv[...].astype(bf16)
                    far_to_mate(s).start()

                @pl.when(n == 1)
                def _():
                    far_to_mate(s).wait_recv()

                    @pl.when(follows)
                    def _():
                        peer_back(s - 1).wait_send()

                    give[1, 0] = (dk[...] + take[s, 0, 0].astype(f32)).astype(bf16)
                    give[1, 1] = (dv[...] + take[s, 0, 1].astype(f32)).astype(bf16)
                    peer_back(s).start()

                @pl.when(n == 2)
                def _():
                    @pl.when(follows)
                    def _():
                        near_to_mate(s - 1).wait_send()
                        fold_o.third()

                    give[0, 0] = dk[...].astype(bf16)
                    give[0, 1] = dv[...].astype(bf16)
                    near_to_mate(s).start()

                first = jnp.where(phase == 1, 1 + n, jnp.where(n == 0, 8, 7 + 2 * n))
                sums.steps(first, jnp.where((phase == 1) | (n == 0), 1, 2))

        @pl.when(phase < seqs)
        def _():
            for wanted in range(seqs):
                at_phase(phase, wanted, [
                    f"{name}{wanted}" for name in ("tok", "attn", "cot", "mixed", "q", "ctx")])
            hidden_stage(phase)
            sums.steps(jnp.where(phase == 0, 0, 5), 1 + phase)

        @pl.when(phase > 0)
        def _():
            at_phase(phase, 1, ["wq", "wk", "wv", "rest"])
            finalize(s)
            sums.steps(jnp.where(phase == 1, 7, 15), 1)

        @pl.when(phase == seqs - 1)
        def _():
            deep = dwo.shape[2]
            total = jnp.zeros((width, dim), f32)
            for r in range(seqs):
                total = total + dot(jnp.transpose(ctx[r]), branch[r])
            for h in range(2):
                for y in range(2):
                    dwo[h, y] = total[h * deep : (h + 1) * deep, y * middle : (y + 1) * middle].astype(bf16)
            fold_o.first()

    begun = 16
    share = dwq.shape[2]

    def square_grad(target, which):
        @pl.loop(0, 4)
        def _(k):
            h, y = k // 2, lax.rem(k, 2)
            target[h, y] = dot(normed_t[rows_at((2 * y + h) * share, share), :], proj[which]).astype(bf16)

    ready("early")
    for n in range(per_tile):
        own = slice(n * chunk, (n + 1) * chunk)
        early[n] = (tok[0, own, :].astype(f32) + attn[n].astype(f32) + early[n].astype(f32)).astype(bf16)
        saving_early(n).start()
    square_grad(dwk, 1)
    fold_k.first()
    sums.steps(begun, 1)
    square_grad(dwv, 2)
    fold_v.first()
    fold_k.second()
    sums.steps(begun + 1, 1)
    square_grad(dwq, 0)
    fold_q.first()
    fold_v.second()
    sums.steps(begun + 2, 1)
    fold_q.second()
    fold_o.fourth()
    sums.steps(begun + 3, 2)
    fold_k.third()
    sums.steps(begun + 5, 1)
    fold_v.third()
    sums.steps(begun + 6, 1)
    fold_q.third()
    fold_k.fourth()
    sums.steps(begun + 7, 1)
    fold_v.fourth()
    sums.steps(begun + 8, 1)
    fold_q.fourth()
    for fold in (fold_o, fold_k, fold_v):
        fold.last()
    sums.steps(begun + 9, count - begun - 9)
    fold_q.last()
    sums.settled(0, count)
    sums.close(count)
    if split:
        me = 4 * side + ring
        gain_all[me] = gain_part[side]

        def share_gain(n):
            dy, dc = others[n]
            y = lax.rem(side + dy, 2)
            return remote(gain_part.at[y], gain_all.at[me], gain_send.at[n], gain_recv.at[n], group[n])

        for n in range(7):
            share_gain(n).start()
        for n in range(7):
            share_gain(n).wait()
        total = gain_all[0]
        for n in range(1, 8):
            total = total + gain_all[n]
        gain_out[...] = total
    else:
        gain_out[...] = gain_part[...]
    for fold in (fold_o, fold_k, fold_v, fold_q):
        fold.settle()
    for copy in (far_to_mate, peer_back, near_to_mate):
        copy(seqs - 1).wait_send()

    for n in range(per_tile):
        saving_early(n).wait()

    @pl.loop(0, count)
    def _(i):
        @pl.when(is_block(i))
        def _():
            saving_block(i, block_of(i)).wait()

        @pl.when(jnp.logical_not(is_block(i)))
        def _():
            saving_token(i, token_of(i)).wait()


def back(split, tok, cot, sums, attn, late, gains, square, q, kv, ctx, lse, cosine, sine, prefix):
    seqs, rows, dim = tok.shape
    width = q.shape[2]
    heads = width // HEAD_DIM
    _, chunk, _ = sums.shape
    tokens = seqs * rows
    early = 256 // chunk
    count = 2 * tokens // chunk - early
    vmem = pl.BlockSpec(memory_space=pltpu.VMEM)
    anyw = pl.BlockSpec(memory_space=pl.ANY)
    dma = pltpu.SemaphoreType.DMA
    lines = pltpu.VMEM((count, chunk, dim), bf16)
    half_lines = pltpu.VMEM((tokens // chunk, chunk, dim), bf16)
    wide = pltpu.VMEM((heads // 2, 2 * rows, width), bf16)
    tall = pltpu.VMEM((heads // 2, width, 2 * rows), bf16)
    shape = jax.ShapeDtypeStruct
    fold_scratch, fold_outs = fold_shapes([(width // 2, dim // 2)] + [(dim // 4, width)] * 3, split)
    loaded = (tok, cot) + tuple(square) + (q, kv, ctx)
    return pl.pallas_call(
        functools.partial(back_kernel, split),
        name="back",
        out_shape=[
            shape((seqs, rows, dim), bf16), shape((seqs, rows, dim), f32), shape((seqs, rows, width), f32),
            shape((8, dim // 2) if split else (2, 8, dim // 2), f32)] + fold_outs,
        in_specs=[anyw] * 12 + [vmem] * 4 + [pl.BlockSpec(memory_space=pltpu.SMEM)],
        out_specs=[anyw, anyw, vmem, vmem] + [anyw] * 4,
        scratch_shapes=[pltpu.VMEM(x.shape, bf16) for x in loaded] + [
            half_lines, half_lines, pltpu.VMEM((early, chunk, dim), bf16),
            pltpu.VMEM((seqs, rows, dim), f32),
            pltpu.VMEM((seqs, rows, dim), bf16),
            tall, wide, tall, wide,
            pltpu.VMEM((width, rows), bf16),
            pltpu.VMEM((heads // 2, 1, 2 * rows), f32),
            pltpu.VMEM((width, rows), f32),
            pltpu.VMEM((rows, width), f32),
            pltpu.VMEM((rows, width), f32),
            pltpu.VMEM((3, 2, rows, width), bf16),
            pltpu.VMEM((seqs, 3, 2, rows, width), bf16),
            pltpu.VMEM((3, tokens, width), bf16),
            pltpu.VMEM((dim, tokens), bf16),
            lines, lines, lines,
            pltpu.VMEM((2, 8, dim // 2), f32),
            pltpu.VMEM((8, 8, dim // 2), f32),
            dma((3,)), dma((seqs, 3)),
            dma((count,)), dma((count,)), dma((count,)), dma((count,)), dma((count + early,)),
            dma((7,)), dma((7,)), dma((8 * seqs + 8,)),
        ] + fold_scratch,
        compiler_params=limits(2, 62),
        cost_estimate=pl.CostEstimate(flops=30 * 10**9, bytes_accessed=10**7, transcendentals=10**7),
    )(late, sums, attn, *loaded, gains, lse, cosine, sine, prefix)


def frequencies():
    half = HEAD_DIM // 2
    lane = np.arange(128) % half
    return np.broadcast_to((rope_base ** (-lane / half)).astype(np.float32), (8, 128))


def halves(weight):
    rows, columns = weight.shape
    return jnp.swapaxes(weight.reshape(rows, 2, columns // 2), 0, 1)


def shards(
    tokens, first_values, norm1_gain, norm2_gain, w_query, w_key, w_value, w_out, w_gate, w_up, w_down,
    prefix, cotangent,
):
    split = lax.axis_size("fsdp") == 2
    seqs, rows, dim = tokens.shape
    width, units = w_query.shape[1], w_gate.shape[1]
    gather = functools.partial(lax.all_gather, axis_name="fsdp", tiled=True)
    if split:
        gains = (norm1_gain, norm2_gain)
        square = (w_query, w_key, w_value, w_out)
        wide = (w_gate.T, w_up.T, w_down)
    else:
        gains = (gather(norm1_gain), gather(norm2_gain))
        square = (gather(w_query), gather(w_key), gather(w_value), halves(gather(w_out, axis=1)))
        wide = (halves(gather(w_gate).T), halves(gather(w_up).T), halves(gather(w_down, axis=1)))
    (sums, late, query, pairs, attn, context, log_total, gain_rows, cosine, sine, down_grad, gate_grad, up_grad,
     *gathered) = front(
        split, tokens, first_values, cotangent, jnp.stack(gains).astype(f32), square, wide, frequencies(), prefix)
    if split:
        square = tuple(gathered)
    block_out, token_grad, half_value_grad, gain_grads, out_grad, key_grad, value_grad, query_grad = back(
        split, tokens, cotangent, sums, attn, late, gain_rows, square, query, pairs, context.reshape(query.shape),
        log_total, cosine, sine, prefix)
    if split:
        over_rows = lambda grad: grad.reshape(-1, grad.shape[-1])
        over_columns = over_rows
        over_turned = lambda grad: over_rows(grad).T
        gain_one_grad, gain_two_grad = gain_grads[0], gain_grads[1]
    else:
        total = lambda grad, axis: lax.psum(
            lax.psum_scatter(grad, "fsdp", scatter_dimension=axis, tiled=True), "ctx").astype(f32)
        over_rows = lambda grad: total(jnp.swapaxes(grad, 0, 1).reshape(-1, grad.shape[-1]), 0)
        over_columns = lambda grad: total(
            jnp.transpose(grad, (0, 2, 1, 3)).reshape(2 * grad.shape[2], -1), 1)
        over_turned = lambda grad: over_columns(grad).T
        gain_one_grad, gain_two_grad = (total(gain_grads[:, n].reshape(-1), 0) for n in range(2))
    return (
        block_out,
        token_grad,
        half_value_grad,
        gain_one_grad,
        gain_two_grad,
        over_rows(query_grad),
        over_rows(key_grad),
        over_rows(value_grad),
        over_columns(out_grad),
        over_turned(gate_grad),
        over_turned(up_grad),
        over_columns(down_grad),
    )


def solution(mesh):
    return jax.shard_map(
        shards,
        mesh=mesh,
        in_specs=(
            P("fsdp", "ctx", None),
            P("fsdp", "ctx", "tp"),
            P("fsdp"),
            P("fsdp"),
            P("fsdp", "tp"),
            P("fsdp", "tp"),
            P("fsdp", "tp"),
            P("tp", "fsdp"),
            P("fsdp", "tp"),
            P("fsdp", "tp"),
            P("tp", "fsdp"),
            P("fsdp"),
            P("fsdp", "ctx", None),
        ),
        out_specs=(
            P("fsdp", "ctx", None),
            P("fsdp", "ctx", None),
            P("fsdp", "ctx", "tp"),
            P("fsdp"),
            P("fsdp"),
            P("fsdp", "tp"),
            P("fsdp", "tp"),
            P("fsdp", "tp"),
            P("tp", "fsdp"),
            P("fsdp", "tp"),
            P("fsdp", "tp"),
            P("tp", "fsdp"),
        ),
        check_vma=False,
    )
```

profile of v0, /device:TPU:0, one launch (start us, length us, event | category | flops | bytes accessed | tf_op | source)
XLA Modules:
  0.0 281.0 jit_solution(16992023059018269970)
XLA Ops:
  0.6 0.7 stack.9
  1.3 0.7 stack.10
  2.0 0.6 maximum_convert_fusion.refs_3_
  2.6 1.2 jit_solution_.3.refs_11_
  3.9 148.4 %front.1 = (bf16[20,64,1024]{2,1,0:T(8,128)(2,1)}, bf16[12,64,1024]{2,1,0:T(8,128)(2,1)}, bf16[2,512,256]{2,1,0:T(8,128)(2,1)}, bf16[2,4,2,512,256]{4,3,2,1,0:T(...) custom-call(bf16[2,512,1024]{2,1,0:T(8,128)(2,1)} %refs_3_.1, ...), custom_call_target="tpu_custom_call" | custom-call | flops 22000001024 | bytes 20000000 | tf_op jit(solution)/shard_map/front/pallas_call | solution.py:812
  152.2 113.5 %back.1 = (bf16[2,512,1024]{2,1,0:T(8,128)(2,1)}, f32[2,512,1024]{2,1,0:T(8,128)}, f32[2,512,256]{2,1,0:T(8,128)}, f32[8,512]{1,0:T(8,128)}, f32[2,128,512]{2,1,...) custom-call(bf16[12,64,1024]{2,1,0:T(8,128)(2,1)} %get-tuple-element.37.refs_0_, ...), custom_call_target="tpu_custom_call" | custom-call | flops 30000001024 | bytes 10000000 | tf_op jit(solution)/shard_map/back/pallas_call | solution.py:1203
  265.7 1.4 fusion
  267.1 0.0 copy-start
  267.1 3.2 %copy.36 = bf16[2,512,1024]{2,1,0:T(8,128)(2,1)} copy(bf16[2,512,1024]{2,1,0:T(8,128)(2,1)} %get-tuple-element.76) | data formatting | bytes 4194304
  270.3 0.0 copy-done
  270.4 0.0 copy-start.4
  270.4 2.0 copy.37
  272.4 0.0 copy-done.4
  272.4 0.0 copy-start.8
  272.4 0.0 copy-start.7
  272.4 0.0 copy-start.6
  272.4 1.0 copy.38
  273.4 0.4 copy-done.8
  273.7 0.0 copy-start.5
  273.7 0.8 copy.39
  274.5 0.0 copy-done.7
  274.5 0.8 copy.40
  275.3 0.0 copy-done.6
  275.3 0.8 copy.41
  276.1 0.0 copy-done.5
  276.1 0.8 copy.42
  276.9 0.0 copy-done.3
  276.9 1.1 copy.43
  278.0 0.0 copy-done.2
  278.0 1.1 copy.44
  279.1 0.8 copy-done.1
  279.9 1.1 copy.45
  (3 shorter events, 0.0 us)
Async XLA Ops:
  267.1 3.2 %copy-start = (f32[2,512,1024]{2,1,0:T(8,128)S(1)}, f32[2,512,1024]{2,1,0:T(8,128)}, u32[]{:S(2)}) copy-start(f32[2,512,1024]{2,1,0:T(8,128)} %get-tuple-element.77) | copy-start | bytes 12582916
  270.4 2.0 copy-start.4
  272.4 1.4 copy-start.8
  272.4 2.2 copy-start.7
  272.4 3.0 %copy-start.6 = (f32[2,256,256]{2,1,0:T(8,128)S(1)}, f32[2,256,256]{2,1,0:T(8,128)}, u32[]{:S(2)}) copy-start(f32[2,256,256]{2,1,0:T(8,128)} %get-tuple-element.57) | copy-start | bytes 1572868
  273.7 2.4 copy-start.5
  273.7 3.2 %copy-start.3 = (f32[2,352,512]{2,1,0:T(8,128)S(1)}, f32[2,352,512]{2,1,0:T(8,128)}, u32[]{:S(2)}) copy-start(f32[2,352,512]{2,1,0:T(8,128)} %get-tuple-element.59) | copy-start | bytes 4325380
  276.1 1.9 copy-start.2
  278.0 1.9 copy-start.1
where the time goes:
time: 281 us
  Pallas kernels  262 us (93%)
  local copies, waits for them, and re-layouts  17.9 us (6%)
    pallas_call x1, Pallas kernels, front(): pl.pallas_call(functools.partial(front_kernel, split), name='front', out_...  148 us
    pallas_call x1, Pallas kernels, back(): pl.pallas_call(functools.partial(back_kernel, split), name='back', out_sh...  113 us
    unnamed x28, local copies, waits for them, and re-layouts  13.9 us

commit v1 on v0

--- a/solution.py
+++ b/solution.py
@@ -2,7 +2,6 @@
 
 import jax
 import jax.numpy as jnp
-import numpy as np
 from jax import lax
 from jax.experimental import pallas as pl
 from jax.experimental.pallas import tpu as pltpu
@@ -198,62 +197,73 @@
 
 
 class Fold:
-    def __init__(self, side, ring, grad, refs, sems, saved, ahead=None):
-        self.ahead = ahead
+    def __init__(self, side, ring, refs, sems, saved):
         self.side, self.half = side, lax.rem(ring, 2)
-        self.grad = grad
-        self.one, self.two, self.three, self.final, self.wide = refs
+        self.grad, self.one, self.two, self.three, self.final = refs
         self.send, self.recv, self.save = sems
         self.mate, self.peer, self.other = (
             {"ctx": near(ring)}, {"ctx": lax.rem(ring + 2, 4)}, {"fsdp": 1 - side})
         self.saved = saved
+        self.began = set()
+
+    def mine(self):
+        return self.grad if self.one is None else self.grad.at[self.half, self.side]
 
     def copy(self, n):
         source, target, device = (
-            (self.grad.at[1 - self.half], self.one, self.mate),
-            (self.grad.at[self.half, 1 - self.side], self.two, self.other),
-            (self.grad.at[self.half, self.side], self.three, self.peer),
-            (self.final.at[self.half], self.final.at[self.half], self.mate),
-        )[n]
+            lambda: (self.grad.at[1 - self.half], self.one, self.mate),
+            lambda: (self.grad.at[self.half, 1 - self.side], self.two, self.other),
+            lambda: (self.mine(), self.three, self.peer),
+            lambda: (self.final.at[self.half], self.final.at[self.half], self.mate),
+        )[n]()
         return remote(source, target, self.send.at[n], self.recv.at[n], device)
 
+    def begin(self, n):
+        self.began.add(n)
+        self.copy(n).start()
+
     def first(self):
-        self.copy(0).start()
+        self.begin(0)
 
     def second(self):
         self.copy(0).wait_recv()
         for side in range(2):
             self.grad[self.half, side] = (
                 self.grad[self.half, side].astype(f32) + self.one[side].astype(f32)).astype(bf16)
-        self.copy(1).start()
+        self.begin(1)
+
+    def join(self):
+        self.copy(1).wait_recv()
+        mine = self.mine()
+        mine[...] = (mine[...].astype(f32) + self.two[...].astype(f32)).astype(bf16)
+
+    def quarter(self):
+        self.join()
+        self.saving().start()
+
+    def resume(self):
+        self.begin(2)
 
     def third(self):
-        self.copy(1).wait_recv()
-        self.grad[self.half, self.side] = (
-            self.grad[self.half, self.side].astype(f32) + self.two[...].astype(f32)).astype(bf16)
-        self.copy(2).start()
+        self.join()
+        self.resume()
 
     def fourth(self):
         self.copy(2).wait_recv()
-        self.final[self.half] = (
-            self.grad[self.half, self.side].astype(f32) + self.three[...].astype(f32)).astype(bf16)
-        self.copy(3).start()
+        self.final[self.half] = (self.mine()[...].astype(f32) + self.three[...].astype(f32)).astype(bf16)
+        self.begin(3)
 
     def saving(self):
-        return pltpu.make_async_copy(self.wide, self.saved, self.save)
+        return pltpu.make_async_copy(self.mine() if self.final is None else self.final, self.saved, self.save)
 
     def last(self):
         self.copy(3).wait_recv()
-        if self.ahead is not None:
-            self.ahead.saving().wait()
-        self.wide[...] = self.final[...].astype(f32)
         self.saving().start()
 
-    def settle(self, saving=True):
-        for n in range(4):
+    def settle(self):
+        for n in sorted(self.began):
             self.copy(n).wait_send()
-        if saving:
-            self.saving().wait()
+        self.saving().wait()
 
 
 class Whole:
@@ -266,45 +276,41 @@
     def second(self):
         pass
 
-    third = fourth = last = second
-
-    def settle(self, saving=True):
+    third = fourth = last = quarter = second
+
+    def settle(self):
         self.copy().wait()
 
 
-def fold_shapes(shapes, split, shared=False):
+def fold_shapes(shapes, split, kinds):
     scratch = []
-    for n, (r, c) in enumerate(shapes):
-        scratch.append(pltpu.VMEM((2, 2, r, c), bf16))
-        if split:
-            scratch += [pltpu.VMEM((2, r, c), bf16), pltpu.VMEM((r, c), bf16), pltpu.VMEM((r, c), bf16),
-                        pltpu.VMEM((2, r, c), bf16)]
-            if n == 0 or not shared:
-                scratch.append(pltpu.VMEM((2, r, c), f32))
+    for r, c in shapes:
+        sizes = ((2, 2, r, c), (2, r, c), (r, c), (r, c), (2, r, c))
+        if not split:
+            kinds = (0,)
+        elif 0 not in kinds:
+            scratch.append(pltpu.VMEM((r, c), bf16))
+        scratch += [pltpu.VMEM(sizes[kind], bf16) for kind in kinds]
     n = len(shapes)
     dma = pltpu.SemaphoreType.DMA
     scratch += [dma((n, 4)), dma((n, 4)), dma((n,))]
-    outs = [
-        jax.ShapeDtypeStruct((2, r, c), f32) if split else jax.ShapeDtypeStruct((2, 2, r, c), bf16)
-        for r, c in shapes]
-    return scratch, outs
-
-
-def make_folds(split, side, ring, scratch, saved, shared=False):
+    ends = (2, 2) if not split else (2,) if 4 in kinds else ()
+    return scratch, [jax.ShapeDtypeStruct(ends + (r, c), bf16) for r, c in shapes]
+
+
+def make_folds(split, side, ring, scratch, saved, kinds):
     send, recv, save = scratch[-3:]
     folds, grads = [], []
-    at = 0
+    per = 1 if not split else len(kinds) + (0 not in kinds)
     for n, target in enumerate(saved):
+        own = list(scratch[n * per : (n + 1) * per])
         sems = (send.at[n], recv.at[n], save.at[n])
-        grads.append(scratch[at])
-        if not split:
-            folds.append(Whole(scratch[at], sems, target))
-            at += 1
-            continue
-        own_wide = n == 0 or not shared
-        refs = list(scratch[at + 1 : at + 5]) + [scratch[at + 5] if own_wide else scratch[5]]
-        folds.append(Fold(side, ring, scratch[at], refs, sems, target, None if own_wide else folds[-1]))
-        at += 6 if own_wide else 5
+        grads.append(own[0])
+        if split:
+            held = dict(zip(kinds if 0 in kinds else (0,) + kinds, own))
+            folds.append(Fold(side, ring, [held.get(kind) for kind in range(5)], sems, target))
+        else:
+            folds.append(Whole(own[0], sems, target))
     return folds, grads
 
 
@@ -327,15 +333,19 @@
             owner == h, values_t, 0.0).astype(bf16)
 
 
+def flat_row(folded):
+    return jnp.concatenate([folded[n : n + 1, :].astype(f32) for n in range(folded.shape[0])], axis=1)
+
+
 def gain_row(gains, which):
     return jnp.concatenate([gains[0, which : which + 1, :], gains[1, which : which + 1, :]], axis=1)
 
 
 def front_kernel(split, *refs):
     place, ring, side = lax.axis_index("tp"), lax.axis_index("ctx"), lax.axis_index("fsdp")
-    (tok, fv, cot_hbm, gain_in, wq_in, wk_in, wv_in, wo_in, wg_in, wu_in, wd_in), refs = refs[:11], refs[11:]
-    (frequency, prefix, sum_hbm, late_hbm, q_out, kv_hbm, attn_hbm, ctx_hbm, lse_out, gains, cosine, sine), refs = (
-        refs[:12], refs[12:])
+    (tok, fv, cot_hbm, g1, g2, wq_in, wk_in, wv_in, wo_in, wg_in, wu_in, wd_in), refs = refs[:12], refs[12:]
+    (prefix, sum_hbm, late_hbm, q_out, kv_hbm, attn_hbm, ctx_hbm, lse_out, gains, cosine, sine), refs = (
+        refs[:11], refs[11:])
     saved, refs = refs[:3], refs[3:]
     if split:
         (wq_hbm, wk_hbm, wv_hbm, wo_hbm), refs = refs[:4], refs[4:]
@@ -346,7 +356,7 @@
      kv_send, kv_recv, kv_save, send_one, recv_one, send_two, recv_two, save,
      wg, wu, wd, loads, cot, inner_t, gg_t, ug_t, late, late_save, wo_all, ctx_all, attn,
      p_send, p_recv, c_send, c_recv, c_save, a_save), refs = refs[:37], refs[37:]
-    (fold_d, fold_g, fold_u), grads = make_folds(split, side, ring, refs, saved, True)
+    (fold_d, fold_g, fold_u), grads = make_folds(split, side, ring, refs, saved, (0, 1, 2))
     seqs, rows, width = q_out.shape
     heads = width // HEAD_DIM
     tile = 256
@@ -372,7 +382,8 @@
 
     if split:
         other = {"fsdp": 1 - side}
-        gains[side, 0:2, :] = gain_in[...]
+        for n, gain in enumerate((g1, g2)):
+            gains[side, n : n + 1, :] = flat_row(gain)
         move_gains = remote(gains.at[side], gains.at[side], g_sems.at[0], g_sems.at[1], other)
         move_gains.start()
 
@@ -405,7 +416,7 @@
         saves = tuple(
             pltpu.make_async_copy(full, target, w_save.at[n])
             for n, (full, target) in enumerate(((wk, wk_hbm), (wv, wv_hbm), (wq, wq_hbm), (wo_all.at[place], wo_hbm))))
-        for n in (0, 1, 3):
+        for n in range(3):
             cross(n).start()
         for own, full, _ in table[:3]:
             full[rows_at(side * own.shape[0], own.shape[0]), :] = own[...]
@@ -425,7 +436,8 @@
     else:
         size = gains.shape[2]
         for piece in range(2):
-            gains[piece, 0:2, :] = gain_in[:, piece * size : (piece + 1) * size]
+            for n, gain in enumerate((g1, g2)):
+                gains[piece, n : n + 1, :] = flat_row(gain)[:, piece * size : (piece + 1) * size]
         wo_all[place] = wo_in[...]
         pass_o = Passing(place, lambda piece, item: wo_all.at[piece, item], (p_send, p_recv))
         pass_o.begin(0)
@@ -434,17 +446,30 @@
     for load in own_loads:
         load.start()
 
-    def pass_block(s, source, target, device, slot):
-        return remote(kv.at[s, source], kv.at[s, target], kv_send.at[s, slot], kv_recv.at[s, target], device)
-
-    to_mate = lambda s: pass_block(s, 0, 1, mate, 0)
-    to_peer = lambda s: pass_block(s, 0, 2, peer, 1)
-    onward = lambda s: pass_block(s, 2, 3, mate, 2)
+    def pass_block(s, which, source, target, device, slot):
+        return remote(
+            kv.at[s, source, which], kv.at[s, target, which], kv_send.at[s, which, slot],
+            kv_recv.at[s, which, target], device)
+
+    to_mate = lambda s, which: pass_block(s, which, 0, 1, mate, 0)
+    to_peer = lambda s, which: pass_block(s, which, 0, 2, peer, 1)
+    onward = lambda s, which: pass_block(s, which, 2, 3, mate, 2)
     gain_one = gain_row(gains, 0)
-    position = (ring * rows + lax.broadcasted_iota(jnp.int32, cosine.shape, 0)).astype(f32)
-    angles = position * frequency[0:1, :]
-    cosine[...] = jnp.cos(angles)
-    sine[...] = jnp.sin(angles) * jnp.where(low_half(cosine.shape), -1.0, 1.0)
+    fine = 16
+    coarse_at = (ring * rows + fine * lax.broadcasted_iota(jnp.int32, (rows // fine, 128), 0)).astype(f32)
+    fine_at = lax.broadcasted_iota(jnp.int32, (fine, 128), 0).astype(f32)
+    step = lax.rem(lax.broadcasted_iota(jnp.int32, (1, 128), 1), HEAD_DIM // 2)
+    frequency = jnp.ones((1, 128), f32)
+    for bit in range(5):
+        ratio = rope_base ** (-(2**bit) / (HEAD_DIM // 2))
+        frequency = frequency * jnp.where(lax.rem(step // 2**bit, 2) == 1, ratio, 1.0)
+    turns = [at * frequency for at in (coarse_at, fine_at)]
+    (cos_a, sin_a), (cos_b, sin_b) = ((jnp.cos(x), jnp.sin(x)) for x in turns)
+    cos_a, sin_a = cos_a[:, None, :], sin_a[:, None, :]
+    cos_b, sin_b = cos_b[None], sin_b[None]
+    cosine[...] = (cos_a * cos_b - sin_a * sin_b).reshape(rows, 128)
+    sine[...] = (sin_a * cos_b + cos_a * sin_b).reshape(rows, 128) * jnp.where(
+        low_half((rows, 128)), -1.0, 1.0)
 
     per_seq_tiles = rows // tile
     tiles = seqs * per_seq_tiles
@@ -457,35 +482,41 @@
         s, at = tile_at(t)
         normed_s[s, at, :] = (unit_norm(tok[s, at, :].astype(f32)) * gain_one).astype(bf16)
 
+    def keys(s):
+        @pl.loop(0, per_seq_tiles)
+        def _(t):
+            at = rows_at(t * tile, tile)
+            k = dot(normed_s[s, at, :], wk[...])
+            kv[s, 0, 0, at, :] = turn(k, cosine[at, :], sine[at, :]).astype(bf16)
+
+        to_peer(s, 0).start()
+        to_mate(s, 0).start()
+
+    def values(s):
+        @pl.loop(0, per_seq_tiles)
+        def _(t):
+            at = rows_at(t * tile, tile)
+            v = dot(normed_s[s, at, :], wv[...])
+            kv[s, 0, 1, at, :] = (0.5 * v + 0.5 * fv[s, at, :].astype(f32)).astype(bf16)
+
+        to_peer(s, 1).start()
+        to_mate(s, 1).start()
+
     if split:
         hand_on(0)
+        onto_mate(0).wait_recv()
+    keys(0)
+    if split:
         hand_on(1)
-        cross(2).start()
-        pass_o.step(0, 1)
-        onto_mate(0).wait_recv()
+        cross(3).start()
         onto_mate(1).wait_recv()
-
-    @pl.loop(0, tiles)
-    def _(t):
-        s, at = tile_at(t)
-        normed = normed_s[s, at, :]
-        k = dot(normed, wk[...])
-        kv[s, 0, 0, at, :] = turn(k, cosine[at, :], sine[at, :]).astype(bf16)
-        v = dot(normed, wv[...])
-        kv[s, 0, 1, at, :] = (0.5 * v + 0.5 * fv[s, at, :].astype(f32)).astype(bf16)
-
-        @pl.when(lax.rem(t, per_seq_tiles) == per_seq_tiles - 1)
-        def _():
-            to_peer(s).start()
-            to_mate(s).start()
-
-    if split:
-        hand_on(3)
-        pass_o.step(0, 2)
-        pass_o.begin(1)
+    values(0)
+    if split:
         hand_on(2)
-        for n in range(4, 7):
-            cross(n).start()
+    for s in range(1, seqs):
+        keys(s)
+        values(s)
+    if split:
         onto_mate(2).wait_recv()
 
     @pl.loop(0, tiles)
@@ -496,11 +527,12 @@
         q_out[s, at, :] = q.astype(bf16)
         spread(qtm.at[s], jnp.transpose(q), lax.rem(t, per_seq_tiles) * tile, rows)
 
-    if not split:
-        pass_o.step(0, 1)
-        pass_o.step(0, 2)
-    pass_o.step(0, 3)
-    pass_o.step(1, 1)
+    pass_o.step(0, 1)
+    if split:
+        hand_on(3)
+        pass_o.begin(1)
+        for n in range(4, 7):
+            cross(n).start()
 
     def saving(i):
         return pltpu.make_async_copy(part.at[i], sum_hbm.at[i], save.at[i])
@@ -526,16 +558,37 @@
         def _(j):
             @pl.when(j == 1)
             def _():
-                to_mate(s).wait_recv()
+                for which in range(2):
+                    to_mate(s, which).wait_recv()
+
+                @pl.when(s > 0)
+                def _():
+                    pass_o.step(1, 2)
 
             @pl.when(j == 2)
             def _():
-                to_peer(s).wait_recv()
-                onward(s).start()
+                for which in range(2):
+                    to_peer(s, which).wait_recv()
+                    onward(s, which).start()
+
+                @pl.when(s == 0)
+                def _():
+                    pass_o.step(0, 2)
+                    pass_o.step(1, 1)
 
             @pl.when(j == 3)
             def _():
-                onward(s).wait_recv()
+                for which in range(2):
+                    onward(s, which).wait_recv()
+
+                @pl.when(s > 0)
+                def _():
+                    pass_o.step(0, 3)
+                    pass_o.step(1, 3)
+                    if split:
+                        for n in range(3):
+                            share_o(n).start()
+                        hand_on(6)
 
             vt[...] = jnp.transpose(kv[s, j, 1])
             key_pos = block_place(ring, j) * rows + lax.broadcasted_iota(jnp.int32, (rows, 1), 0)
@@ -558,10 +611,11 @@
                     acct[of_head, :] = acct[of_head, :] * fade[:, lanes] + dot(vt[of_head, :], low[:, lanes])
                 at_step = j * (heads // 2) + h
 
-                @pl.when((s > 0) & (at_step < 3 * per_seq_tiles))
+                n = jnp.where(at_step == 7, 3, at_step // 2 - 1)
+
+                @pl.when((s > 0) & (at_step > 1) & ((at_step == 7) | (lax.rem(at_step, 2) == 0)))
                 def _():
-                    passing.step(
-                        (s - 1) * per_seq_tiles + lax.rem(at_step, per_seq_tiles), 1 + at_step // per_seq_tiles)
+                    passing.step((s - 1) * per_seq_tiles + lax.rem(n, per_seq_tiles), 1 + n // per_seq_tiles)
 
         for h in range(heads):
             if h % 2 == 0:
@@ -570,14 +624,12 @@
             acct[of_head, :] = acct[of_head, :] / totals[h // 2][:, h % 2 * rows : (h % 2 + 1) * rows]
         for t in range(per_seq_tiles):
             ctx_all[place, s * per_seq_tiles + t] = jnp.transpose(acct[:, t * tile : (t + 1) * tile]).astype(bf16)
-        for t in range(per_seq_tiles):
             passing.begin(s * per_seq_tiles + t)
         saving_context(s).start()
         saving_kv(s).start()
 
         @pl.when(s == 0)
         def _():
-            pass_o.step(1, 2)
             if split:
                 onto_mate(3).wait_recv()
                 for copy in saves:
@@ -586,11 +638,6 @@
                 hand_on(5)
 
     if split:
-        hand_on(6)
-    pass_o.step(1, 3)
-    if split:
-        for n in range(3):
-            share_o(n).start()
         for n in range(3):
             share_o(n).wait_recv()
     if split:
@@ -614,24 +661,27 @@
         mine = pl.ds((t - 1) * per_tile, per_tile)
         return pltpu.make_async_copy(late.at[mine], late_hbm.at[mine], late_save.at[t - 1])
 
-    @pl.loop(0, tiles)
-    def _(t):
-        s, at = tile_at(t)
-        flat = rows_at(t * tile, tile)
+    stepped = [0]
+
+    def act(*plan):
+        for what in plan:
+            if what == "sum":
+                sums.steps(stepped[0], 1)
+                stepped[0] += 1
+            else:
+                passing.step(*what)
+
+    plans = {
+        (0, 0): [(0, 3)], (0, 1): [(1, 3)], (0, 2): [(2, 1)], (0, 3): [],
+        (1, 0): [], (1, 1): [(3, 1)], (1, 2): [], (1, 3): ["sum"],
+        (2, 0): [(2, 2), "sum", (3, 2), "sum", (2, 3)], (2, 1): ["sum"], (2, 2): [], (2, 3): ["sum"],
+        (3, 0): [(3, 3)], (3, 1): ["sum"], (3, 2): ["sum"], (3, 3): ["sum"],
+    }
+    for t in range(tiles):
+        s, at = t // per_seq_tiles, slice(t % per_seq_tiles * tile, (t % per_seq_tiles + 1) * tile)
+        flat = slice(t * tile, (t + 1) * tile)
         mine = t * per_tile
-
-        def tick(n):
-            at_step = 3 * t + n
-
-            @pl.when(t < per_seq_tiles)
-            def _():
-                passing.step(
-                    (seqs - 1) * per_seq_tiles + lax.rem(at_step, per_seq_tiles), 1 + at_step // per_seq_tiles)
-
-            @pl.when((t >= per_seq_tiles) & (n > 0))
-            def _():
-                sums.steps(2 * (t - per_seq_tiles) + n - 1, 1)
-
+        act(*plans[t, 0])
         context = jnp.concatenate([ctx_all[p, t] for p in range(4)], axis=1)
         attended = [
             dot(context, jnp.concatenate([wo_all[p, piece] for p in range(4)], axis=0)) for piece in range(2)]
@@ -652,20 +702,17 @@
         inner_grad = across_both(cot[s, at, :], wd)
         gate_grad = (inner_grad * up * sigmoid * (1.0 + gate * (1.0 - sigmoid))).astype(bf16)
         up_grad = (inner_grad * swish).astype(bf16)
-        tick(0)
+        act(*plans[t, 1])
         for piece in range(2):
             sums.fill(mine, piece, dot(gate_grad, wg[piece]) + dot(up_grad, wu[piece]))
         sums.offer(mine, per_tile)
-        tick(1)
+        act(*plans[t, 2])
         feeds = [dot(inner, wd[piece]) for piece in range(2)]
 
-        @pl.when(t == 0)
-        def _():
+        if t == 0:
             for piece in range(2):
                 sums.fill(early, piece, feeds[piece])
-
-        @pl.when(t > 0)
-        def _():
+        else:
             for piece in range(2):
                 for k in range(per_tile):
                     late[mine - per_tile + k, :, piece * middle : (piece + 1) * middle] = feeds[piece][
@@ -674,7 +721,7 @@
 
         gg_t[:, flat] = jnp.transpose(gate_grad)
         ug_t[:, flat] = jnp.transpose(up_grad)
-        tick(2)
+        act(*plans[t, 3])
 
     sums.offer(early, count - early)
     deep = units // 2
@@ -689,7 +736,7 @@
                         right[s, :, y * middle : (y + 1) * middle])
                 grads[n][h, y] = total.astype(bf16)
 
-    begun = 2 * (tiles - per_seq_tiles)
+    begun = stepped[0]
     weight_grad(0, inner_t, cot)
     fold_d.first()
     sums.steps(begun, 1)
@@ -702,31 +749,23 @@
     fold_g.second()
     sums.steps(begun + 2, 1)
     fold_u.second()
-    sums.steps(begun + 3, 2)
-    fold_d.third()
-    sums.steps(begun + 5, 3)
-    fold_g.third()
-    fold_d.fourth()
-    sums.steps(begun + 8, 3)
-    fold_u.third()
-    fold_g.fourth()
-    fold_d.last()
-    sums.steps(begun + 11, 3)
-    fold_u.fourth()
-    fold_g.last()
-    sums.steps(begun + 14, count - begun - 14)
-    fold_u.last()
+    sums.steps(begun + 3, 3)
+    fold_d.quarter()
+    sums.steps(begun + 6, 3)
+    fold_g.quarter()
+    sums.steps(begun + 9, count - begun - 9)
+    fold_u.quarter()
     sums.settled(0, count)
     sums.close(count)
-    for fold in (fold_d, fold_g):
-        fold.settle(False)
-    fold_u.settle()
+    for fold in (fold_d, fold_g, fold_u):
+        fold.settle()
     for t in range(1, tiles):
         saving_late(t).wait()
     for s in range(seqs):
-        to_mate(s).wait_send()
-        to_peer(s).wait_send()
-        onward(s).wait_send()
+        for which in range(2):
+            to_mate(s, which).wait_send()
+            to_peer(s, which).wait_send()
+            onward(s, which).wait_send()
         saving_kv(s).wait()
         saving_context(s).wait()
     for t in range(tiles):
@@ -753,7 +792,7 @@
         collective_id=ident, has_side_effects=True, vmem_limit_bytes=megabytes * 1024 * 1024)
 
 
-def front(split, tok, fv, cot, gains, square, wide, frequency, prefix):
+def front(split, tok, fv, cot, gains, square, wide, prefix):
     seqs, rows, dim = tok.shape
     width, units = square[0].shape[1], wide[0].shape[-2]
     heads = width // HEAD_DIM
@@ -768,7 +807,7 @@
     lines = pltpu.VMEM((count, chunk, dim), bf16)
     shape = jax.ShapeDtypeStruct
     full = [(dim, width)] * 3 + [(2, width, dim // 2)]
-    fold_scratch, fold_outs = fold_shapes([(units // 2, dim // 2)] * 3, split, True)
+    fold_scratch, fold_outs = fold_shapes([(units // 2, dim // 2)] * 3, split, (0, 1, 2))
     outs = [
         shape((count, chunk, dim), bf16), shape((after, chunk, dim), bf16), shape((seqs, rows, width), bf16),
         shape((seqs, 4, 2, rows, width), bf16), shape((tokens // chunk, chunk, dim), bf16),
@@ -791,7 +830,7 @@
         pltpu.VMEM((heads // 2, 1, 2 * rows), f32),
         pltpu.VMEM((heads // 2, 1, 2 * rows), f32),
         lines, lines, lines,
-        dma((seqs, 3)), dma((seqs, 4)), dma((seqs,)),
+        dma((seqs, 2, 3)), dma((seqs, 2, 4)), dma((seqs,)),
         dma((count,)), dma((count,)), dma((count,)), dma((count,)), dma((count,)),
         pltpu.VMEM((2, padded, dim // 2), bf16),
         pltpu.VMEM((2, padded, dim // 2), bf16),
@@ -813,25 +852,29 @@
         functools.partial(front_kernel, split),
         name="front",
         out_shape=outs,
-        in_specs=[vmem] * 2 + [anyw] + [vmem] * 5 + [anyw] * 3 + [vmem, pl.BlockSpec(memory_space=pltpu.SMEM)],
+        in_specs=[vmem] * 2 + [anyw] + [vmem] * 6 + [anyw] * 3 + [pl.BlockSpec(memory_space=pltpu.SMEM)],
         out_specs=out_specs,
         scratch_shapes=scratch,
         compiler_params=limits(0, 63),
         cost_estimate=pl.CostEstimate(flops=22 * 10**9, bytes_accessed=2 * 10**7, transcendentals=10**7),
-    )(tok, fv, cot, gains, *square, *wide, frequency, prefix)
+    )(tok, fv, cot, *gains, *square, *wide, prefix)
 
 
 def back_kernel(split, *refs):
     place, ring, side = lax.axis_index("tp"), lax.axis_index("ctx"), lax.axis_index("fsdp")
+    quarters, refs = (refs[:3], refs[3:]) if split else ((), refs)
     loaded, refs = refs[:12], refs[12:]
-    (gain_in, lse, cosine, sine, prefix, block_hbm, token_hbm, fv_out, gain_out), saved, refs = (
+    (gain_in, lse, cosine, sine, prefix, block_hbm, token_hbm, fv_hbm, gain_out), saved, refs = (
         refs[:9], refs[9:13], refs[13:])
+    ends_saved, refs = (refs[:3], refs[3:]) if split else ((), refs)
     (tok, cot, wq, wk, wv, wo, q, kv, ctx, attn, mixed, early), refs = refs[:12], refs[12:]
-    (hid, branch, qtm, qm, otm, om, kt, delta, dqt, dk, dv, give, take, proj, normed_t,
+    (hid, dwo_sum, qtm, qm, otm, om, kt, delta, dqt, dk, dv, give, take, proj, normed_t,
      part, inward, across, gain_part, gain_all,
-     kv_send, kv_recv, send_one, recv_one, send_two, recv_two, save, gain_send, gain_recv, loads), refs = (
-        refs[:30], refs[30:])
-    (fold_o, fold_k, fold_v, fold_q), (dwo, dwk, dwv, dwq) = make_folds(split, side, ring, refs, saved)
+     kv_send, kv_recv, send_one, recv_one, send_two, recv_two, save, gain_send, gain_recv, loads, fv_save), refs = (
+        refs[:31], refs[31:])
+    ends_scratch, refs = (refs[:12], refs[12:]) if split else ((), refs)
+    (fold_o, fold_k, fold_v, fold_q), (dwo, dwk, dwv, dwq) = make_folds(split, side, ring, refs, saved, (0, 1, 2, 3, 4))
+    ends, ends_mine = make_folds(split, side, ring, ends_scratch, ends_saved, (3, 4)) if split else ((), ())
     late_hbm, sum_hbm, attn_hbm, tok_hbm, cot_hbm, wq_hbm, wk_hbm, wv_hbm, wo_hbm, q_hbm, kv_hbm, ctx_hbm = loaded
     seqs, rows, dim = tok.shape
     width = wq.shape[1]
@@ -843,7 +886,8 @@
     middle = dim // 2
     lines = seqs * per_seq
     count = 2 * lines - per_tile
-    head_start, rest = per_seq, per_seq - per_tile
+    head_start = per_seq + 2
+    rest = 2 * per_seq - per_tile - head_start
     rest_start = head_start + per_seq
     own_start = (head_start, rest_start + rest)
     mate, peer = ring_peers(ring)
@@ -852,31 +896,38 @@
 
     copies = {}
 
-    def load(name, source, target):
+    def load(name, source, target, start=True):
         copies[name] = pltpu.make_async_copy(source, target, loads.at[len(copies)])
-        copies[name].start()
+        if start:
+            copies[name].start()
 
     def ready(*names):
         for name in names:
             copies[name].wait()
 
     load("late", late_hbm.at[0:head_start], part.at[0:head_start])
+    later = []
     for s in range(seqs):
         mine = slice(s * per_seq, (s + 1) * per_seq)
-        load(f"tok{s}", tok_hbm.at[s], tok.at[s])
-        load(f"attn{s}", attn_hbm.at[mine], attn.at[mine])
-        load(f"cot{s}", cot_hbm.at[s], cot.at[s])
-        load(f"mixed{s}", sum_hbm.at[mine], mixed.at[mine])
+        for name, source, target in (
+            ("tok", tok_hbm.at[s], tok.at[s]), ("attn", attn_hbm.at[mine], attn.at[mine]),
+            ("cot", cot_hbm.at[s], cot), ("mixed", sum_hbm.at[mine], mixed),
+            ("q", q_hbm.at[s], q.at[s]), ("ctx", ctx_hbm.at[s], ctx.at[s]), ("kv", kv_hbm.at[s], kv),
+        ):
+            now = s == 0 and name != "kv"
+            load(f"{name}{s}", source, target, now)
+            if not now and (s == 0 or name not in ("cot", "mixed", "kv")):
+                later.append(f"{name}{s}")
         if s == 0:
             load("wo", wo_hbm, wo)
-        load(f"q{s}", q_hbm.at[s], q.at[s])
-        load(f"ctx{s}", ctx_hbm.at[s], ctx.at[s])
-        load(f"kv{s}", kv_hbm.at[s], kv.at[s])
-    load("rest", late_hbm.at[head_start : head_start + rest], part.at[rest_start : rest_start + rest])
-    load("early", sum_hbm.at[lines : lines + per_tile], early)
-    load("wq", wq_hbm, wq)
-    load("wk", wk_hbm, wk)
-    load("wv", wv_hbm, wv)
+    for name, source, target in (
+        [(f"quarter{n}", quarter, ends_mine[n]) for n, quarter in enumerate(quarters)] + [
+            ("rest", late_hbm.at[head_start : head_start + rest], part.at[rest_start : rest_start + rest]),
+            ("early", sum_hbm.at[lines : lines + per_tile], early),
+            ("wq", wq_hbm, wq), ("wk", wk_hbm, wk), ("wv", wv_hbm, wv)]
+    ):
+        load(name, source, target, False)
+        later.append(name)
     greet(line_peers(place) + (group if split else ring_peers(ring)))
     gain_one, gain_two = gain_row(gain_in, 0), gain_row(gain_in, 1)
     gain_part[...] = jnp.zeros_like(gain_part)
@@ -934,6 +985,8 @@
     near_to_mate = lambda s: move(s, 0, 2, mate)
     ready("late")
     sums.offer(0, head_start)
+    for name in later:
+        copies[name].start()
 
     def hidden_stage(s):
         @pl.loop(0, rows // tile)
@@ -943,15 +996,16 @@
             join = lambda ref: jnp.concatenate([ref[first + k] for k in range(per_tile)], axis=0).astype(f32)
             token = tok[s, at, :].astype(f32)
             values = token + join(attn)
-            upstream = join(mixed)
+            upstream = jnp.concatenate(
+                [mixed[t * per_tile + k] for k in range(per_tile)], axis=0).astype(f32)
             factor = lax.rsqrt(jnp.mean(values * values, axis=-1, keepdims=True) + epsilon)
             scaled = upstream * gain_two
             add_gain(1, jnp.sum(upstream * values * factor, axis=0, keepdims=True))
-            hid_now = cot[s, at, :].astype(f32) + factor * scaled - values * factor**3 * jnp.mean(
+            hid_now = cot[at, :].astype(f32) + factor * scaled - values * factor**3 * jnp.mean(
                 scaled * values, axis=-1, keepdims=True)
             hid[s, at, :] = hid_now
             low = hid_now.astype(bf16)
-            branch[s, at, :] = low
+            dwo_sum[...] += dot(jnp.transpose(ctx[s, at, :]), low)
             left, right = low[:, :middle], low[:, middle:]
             grad = dot_nt(left, wo[0]) + dot_nt(right, wo[1])
             lane_owner = lax.broadcasted_iota(jnp.int32, grad.shape, 1) // HEAD_DIM
@@ -970,8 +1024,8 @@
             normed = (unit_norm(token) * gain_one).astype(bf16)
             normed_t[:, rows_at(s * rows + t * tile, tile)] = jnp.transpose(normed)
 
-    def back_block(s, j):
-        kt[...] = jnp.transpose(kv[s, j, 0])
+    def back_block(s, j, tick):
+        kt[...] = jnp.transpose(kv[j, 0])
         key_pos = block_place(ring, j) * rows + lax.broadcasted_iota(jnp.int32, (rows, 1), 0)
         query_pos = ring * rows + lax.rem(lax.broadcasted_iota(jnp.int32, (1, 2 * rows), 1), rows)
         seen = key_pos < jnp.maximum(query_pos + 1, prefix[s])
@@ -980,15 +1034,16 @@
 
         @pl.loop(0, heads // 2)
         def _(h):
-            scores = dot(kv[s, j, 0], qtm[h])
+            scores = dot(kv[j, 0], qtm[h])
             probs = jnp.where(seen, jnp.exp(scores - lse[s, pl.ds(h, 1), :]), 0.0)
-            dprobs = dot(kv[s, j, 1], otm[h])
+            dprobs = dot(kv[j, 1], otm[h])
             dv[...] += dot(probs.astype(bf16), om[h])
             dscores = (probs * (dprobs - delta[h])).astype(bf16)
             dk[...] += dot(dscores, qm[h])
             for n in range(2):
                 of_head = rows_at((2 * h + n) * HEAD_DIM, HEAD_DIM)
                 dqt[of_head, :] += dot(kt[of_head, :], dscores[:, n * rows : (n + 1) * rows])
+            tick(h)
 
     def finalize(s):
         near_to_mate(s).wait_recv()
@@ -1004,7 +1059,6 @@
             proj[0, flat, :] = turn(grad_q, co, si, -1.0).astype(bf16)
             proj[1, flat, :] = turn(grad_k, co, si, -1.0).astype(bf16)
             proj[2, flat, :] = grad_v.astype(bf16)
-            fv_out[s, at, :] = grad_v
             i = jnp.where(s == 0, own_start[0], own_start[1]) + t * per_tile
             for piece in range(2):
                 cut = slice(piece * middle, (piece + 1) * middle)
@@ -1017,11 +1071,25 @@
             sums.offer(rest_start, rest)
 
     ready("wo")
+    dwo_sum[...] = jnp.zeros_like(dwo_sum)
+    if split:
+        ready("quarter0")
+        ends[0].resume()
+
+    def start_at(phase, *names):
+        for wanted in range(1, seqs):
+            @pl.when(phase == wanted - 1)
+            def _():
+                for name in names:
+                    copies[f"{name}{wanted}"].start()
 
     def at_phase(phase, wanted, names):
         @pl.when(phase == wanted)
         def _():
             ready(*names)
+
+    plan = [(1, m, line) for line, m in enumerate((0, 2, 3, 5, 7))] + [
+        (2, m, 9 + line) for line, m in enumerate((1, 3, 4, 6))]
 
     @pl.loop(0, seqs + 1)
     def _(phase):
@@ -1036,7 +1104,16 @@
 
             @pl.loop(0, 4)
             def _(n):
-                back_block(s, 3 - n)
+                def tick(h):
+                    chosen = -1
+                    for at_phase, at_step, line in plan:
+                        chosen = jnp.where((phase == at_phase) & (2 * n + h == at_step), line, chosen)
+
+                    @pl.when(chosen >= 0)
+                    def _():
+                        sums.steps(chosen, 1)
+
+                back_block(s, 3 - n, tick)
 
                 @pl.when(n == 0)
                 def _():
@@ -1072,8 +1149,7 @@
                     give[0, 1] = dv[...].astype(bf16)
                     near_to_mate(s).start()
 
-                first = jnp.where(phase == 1, 1 + n, jnp.where(n == 0, 8, 7 + 2 * n))
-                sums.steps(first, jnp.where((phase == 1) | (n == 0), 1, 2))
+            start_at(phase - 1, "kv")
 
         @pl.when(phase < seqs)
         def _():
@@ -1081,26 +1157,40 @@
                 at_phase(phase, wanted, [
                     f"{name}{wanted}" for name in ("tok", "attn", "cot", "mixed", "q", "ctx")])
             hidden_stage(phase)
-            sums.steps(jnp.where(phase == 0, 0, 5), 1 + phase)
+            start_at(phase, "cot", "mixed")
+
+            @pl.when(phase == 1)
+            def _():
+                sums.steps(5, 1)
 
         @pl.when(phase > 0)
         def _():
             at_phase(phase, 1, ["wq", "wk", "wv", "rest"])
+            sums.steps(jnp.where(phase == 1, 6, 13), jnp.where(phase == 1, 1, 2))
             finalize(s)
             sums.steps(jnp.where(phase == 1, 7, 15), 1)
 
         @pl.when(phase == seqs - 1)
         def _():
             deep = dwo.shape[2]
-            total = jnp.zeros((width, dim), f32)
-            for r in range(seqs):
-                total = total + dot(jnp.transpose(ctx[r]), branch[r])
             for h in range(2):
                 for y in range(2):
-                    dwo[h, y] = total[h * deep : (h + 1) * deep, y * middle : (y + 1) * middle].astype(bf16)
+                    dwo[h, y] = dwo_sum[h * deep : (h + 1) * deep, y * middle : (y + 1) * middle].astype(bf16)
             fold_o.first()
+            if split:
+                ends[0].fourth()
+                ready("quarter1")
+                ends[1].resume()
+            sums.steps(8, 1)
 
     begun = 16
+    fv_copy = pltpu.make_async_copy(proj.at[2], fv_hbm, fv_save)
+    fv_copy.start()
+    if split:
+        ends[1].fourth()
+        ready("quarter2")
+        ends[2].resume()
+        ends[0].last()
     share = dwq.shape[2]
 
     def square_grad(target, which):
@@ -1138,10 +1228,13 @@
     fold_v.fourth()
     sums.steps(begun + 8, 1)
     fold_q.fourth()
-    for fold in (fold_o, fold_k, fold_v):
+    for fold in (fold_o, fold_k, fold_v) + tuple(ends[1:2]):
         fold.last()
+    if split:
+        ends[2].fourth()
     sums.steps(begun + 9, count - begun - 9)
-    fold_q.last()
+    for fold in (fold_q,) + tuple(ends[2:]):
+        fold.last()
     sums.settled(0, count)
     sums.close(count)
     if split:
@@ -1163,8 +1256,9 @@
         gain_out[...] = total
     else:
         gain_out[...] = gain_part[...]
-    for fold in (fold_o, fold_k, fold_v, fold_q):
+    for fold in (fold_o, fold_k, fold_v, fold_q) + tuple(ends):
         fold.settle()
+    fv_copy.wait()
     for copy in (far_to_mate, peer_back, near_to_mate):
         copy(seqs - 1).wait_send()
 
@@ -1182,7 +1276,7 @@
             saving_token(i, token_of(i)).wait()
 
 
-def back(split, tok, cot, sums, attn, late, gains, square, q, kv, ctx, lse, cosine, sine, prefix):
+def back(split, quarters, tok, cot, sums, attn, late, gains, square, q, kv, ctx, lse, cosine, sine, prefix):
     seqs, rows, dim = tok.shape
     width = q.shape[2]
     heads = width // HEAD_DIM
@@ -1198,20 +1292,23 @@
     wide = pltpu.VMEM((heads // 2, 2 * rows, width), bf16)
     tall = pltpu.VMEM((heads // 2, width, 2 * rows), bf16)
     shape = jax.ShapeDtypeStruct
-    fold_scratch, fold_outs = fold_shapes([(width // 2, dim // 2)] + [(dim // 4, width)] * 3, split)
+    fold_scratch, fold_outs = fold_shapes(
+        [(width // 2, dim // 2)] + [(dim // 4, width)] * 3, split, (0, 1, 2, 3, 4))
+    ends_scratch, ends_outs = fold_shapes([x.shape for x in quarters], True, (3, 4)) if split else ([], [])
     loaded = (tok, cot) + tuple(square) + (q, kv, ctx)
+    held = [tok.shape, cot.shape[1:]] + [x.shape for x in square] + [q.shape, kv.shape[1:], ctx.shape]
     return pl.pallas_call(
         functools.partial(back_kernel, split),
         name="back",
         out_shape=[
-            shape((seqs, rows, dim), bf16), shape((seqs, rows, dim), f32), shape((seqs, rows, width), f32),
-            shape((8, dim // 2) if split else (2, 8, dim // 2), f32)] + fold_outs,
-        in_specs=[anyw] * 12 + [vmem] * 4 + [pl.BlockSpec(memory_space=pltpu.SMEM)],
-        out_specs=[anyw, anyw, vmem, vmem] + [anyw] * 4,
-        scratch_shapes=[pltpu.VMEM(x.shape, bf16) for x in loaded] + [
-            half_lines, half_lines, pltpu.VMEM((early, chunk, dim), bf16),
+            shape((seqs, rows, dim), bf16), shape((seqs, rows, dim), f32), shape((tokens, width), bf16),
+            shape((8, dim // 2) if split else (2, 8, dim // 2), f32)] + fold_outs + ends_outs,
+        in_specs=[anyw] * (len(quarters) + 12) + [vmem] * 4 + [pl.BlockSpec(memory_space=pltpu.SMEM)],
+        out_specs=[anyw, anyw, anyw, vmem] + [anyw] * (4 + len(quarters)),
+        scratch_shapes=[pltpu.VMEM(x, bf16) for x in held] + [
+            half_lines, pltpu.VMEM((rows // chunk, chunk, dim), bf16), pltpu.VMEM((early, chunk, dim), bf16),
             pltpu.VMEM((seqs, rows, dim), f32),
-            pltpu.VMEM((seqs, rows, dim), bf16),
+            pltpu.VMEM((width, dim), f32),
             tall, wide, tall, wide,
             pltpu.VMEM((width, rows), bf16),
             pltpu.VMEM((heads // 2, 1, 2 * rows), f32),
@@ -1227,17 +1324,60 @@
             pltpu.VMEM((8, 8, dim // 2), f32),
             dma((3,)), dma((seqs, 3)),
             dma((count,)), dma((count,)), dma((count,)), dma((count,)), dma((count + early,)),
-            dma((7,)), dma((7,)), dma((8 * seqs + 8,)),
-        ] + fold_scratch,
+            dma((7,)), dma((7,)), dma((8 * seqs + 11,)), dma(()),
+        ] + ends_scratch + fold_scratch,
         compiler_params=limits(2, 62),
         cost_estimate=pl.CostEstimate(flops=30 * 10**9, bytes_accessed=10**7, transcendentals=10**7),
-    )(late, sums, attn, *loaded, gains, lse, cosine, sine, prefix)
-
-
-def frequencies():
-    half = HEAD_DIM // 2
-    lane = np.arange(128) % half
-    return np.broadcast_to((rope_base ** (-lane / half)).astype(np.float32), (8, 128))
+    )(*quarters, late, sums, attn, *loaded, gains, lse, cosine, sine, prefix)
+
+
+def finish_kernel(parts, *refs):
+    n = len(parts)
+    sources, gain_in, refs = refs[:n], refs[n], refs[n + 1 :]
+    targets, gain_one, gain_two, refs = refs[:n], refs[n], refs[n + 1], refs[n + 2 :]
+    held, wide, (loads, saves) = refs[:n], refs[n : 2 * n], refs[2 * n :]
+    loading, saving = [], []
+    for k, count in enumerate(parts):
+        size = sources[k].shape[0] // count
+        for piece in range(count):
+            at = slice(piece * size, (piece + 1) * size)
+            place = len(loading)
+            loading.append(pltpu.make_async_copy(sources[k].at[at], held[k].at[at], loads.at[place]))
+            plain = sources[k].dtype == targets[k].dtype
+            saving.append((k, at, plain, pltpu.make_async_copy(
+                (held if plain else wide)[k].at[at], targets[k].at[at], saves.at[place])))
+    for load in loading:
+        load.start()
+    gain_one[...] = gain_in[0:1, :]
+    gain_two[...] = gain_in[1:2, :]
+    for load, (k, at, plain, save) in zip(loading, saving):
+        load.wait()
+        if not plain:
+            wide[k][at] = held[k][at].astype(f32)
+        save.start()
+    for *_, save in saving:
+        save.wait()
+
+
+def finish(arrays, types, gain_rows):
+    parts = [2 if x.size > 300000 else 1 for x in arrays]
+    vmem = pl.BlockSpec(memory_space=pltpu.VMEM)
+    anyw = pl.BlockSpec(memory_space=pl.ANY)
+    dma = pltpu.SemaphoreType.DMA
+    shape = jax.ShapeDtypeStruct
+    row = shape((1, gain_rows.shape[1]), f32)
+    return pl.pallas_call(
+        functools.partial(finish_kernel, parts),
+        name="finish",
+        out_shape=[shape(x.shape, t) for x, t in zip(arrays, types)] + [row, row],
+        in_specs=[anyw] * len(arrays) + [vmem],
+        out_specs=[anyw] * len(arrays) + [vmem, vmem],
+        scratch_shapes=[pltpu.VMEM(x.shape, x.dtype) for x in arrays] + [
+            pltpu.VMEM((8, 128) if x.dtype == t else x.shape, f32) for x, t in zip(arrays, types)] + [
+            dma((sum(parts),)), dma((sum(parts),))],
+        compiler_params=pltpu.CompilerParams(vmem_limit_bytes=60 * 1024 * 1024),
+        cost_estimate=pl.CostEstimate(flops=10**6, bytes_accessed=25 * 10**6, transcendentals=0),
+    )(*arrays, gain_rows)
 
 
 def halves(weight):
@@ -1263,18 +1403,24 @@
         wide = (halves(gather(w_gate).T), halves(gather(w_up).T), halves(gather(w_down, axis=1)))
     (sums, late, query, pairs, attn, context, log_total, gain_rows, cosine, sine, down_grad, gate_grad, up_grad,
      *gathered) = front(
-        split, tokens, first_values, cotangent, jnp.stack(gains).astype(f32), square, wide, frequencies(), prefix)
+        split, tokens, first_values, cotangent, [gain.reshape(-1, 128) for gain in gains], square, wide, prefix)
     if split:
         square = tuple(gathered)
-    block_out, token_grad, half_value_grad, gain_grads, out_grad, key_grad, value_grad, query_grad = back(
-        split, tokens, cotangent, sums, attn, late, gain_rows, square, query, pairs, context.reshape(query.shape),
-        log_total, cosine, sine, prefix)
-    if split:
+    wide_grads = (down_grad, gate_grad, up_grad)
+    block_out, token_grad, half_value_grad, gain_grads, out_grad, key_grad, value_grad, query_grad, *ends = back(
+        split, wide_grads if split else (), tokens, cotangent, sums, attn, late, gain_rows, square, query, pairs,
+        context.reshape(query.shape), log_total, cosine, sine, prefix)
+    half_value_grad = half_value_grad.reshape(seqs, rows, width)
+    if split:
+        arrays = (token_grad, block_out, half_value_grad, query_grad, key_grad, value_grad, out_grad, *ends)
+        (token_grad, block_out, half_value_grad, query_grad, key_grad, value_grad, out_grad, down_grad, gate_grad,
+         up_grad, gain_one_grad, gain_two_grad) = finish(arrays, (f32, bf16) + (f32,) * 8, gain_grads)
         over_rows = lambda grad: grad.reshape(-1, grad.shape[-1])
         over_columns = over_rows
         over_turned = lambda grad: over_rows(grad).T
-        gain_one_grad, gain_two_grad = gain_grads[0], gain_grads[1]
+        gain_one_grad, gain_two_grad = gain_one_grad[0], gain_two_grad[0]
     else:
+        half_value_grad = half_value_grad.astype(f32)
         total = lambda grad, axis: lax.psum(
             lax.psum_scatter(grad, "fsdp", scatter_dimension=axis, tiled=True), "ctx").astype(f32)
         over_rows = lambda grad: total(jnp.swapaxes(grad, 0, 1).reshape(-1, grad.shape[-1]), 0)

time: 281 us -> 260 us (0.925)
  local copies, waits for them, and re-layouts: 17.9 us -> 0 us
  Pallas kernels: 262 us -> 259 us
    unnamed x28 -> x0, local copies, waits for them, and re-layouts: 13.9 us -> none
    pallas_call x1, Pallas kernels: 148 us -> 135 us  [front(): pl.pallas_call(functools.partial(front_kernel, split), name='front', out_...]
    pallas_call x0 -> x1, Pallas kernels: none -> 9.49 us  [finish(): pl.pallas_call(functools.partial(finish_kernel, parts), name='finish', ou...]
where the time goes in v1:
time: 260 us
  Pallas kernels  259 us (100%)
    pallas_call x1, Pallas kernels, front(): pl.pallas_call(functools.partial(front_kernel, split), name='front', out_...  135 us
    pallas_call x1, Pallas kernels, back(): pl.pallas_call(functools.partial(back_kernel, split), name='back', out_sh...  115 us
    pallas_call x1, Pallas kernels, finish(): pl.pallas_call(functools.partial(finish_kernel, parts), name='finish', ou...  9.49 us

profile of v1, /device:TPU:0, one launch (start us, length us, event | category | flops | bytes accessed | tf_op | source)
XLA Modules:
  0.0 260.2 jit_solution(2472108154439359813)
XLA Ops:
  0.6 134.7 %front.1 = (bf16[20,64,1024]{2,1,0:T(8,128)(2,1)}, bf16[12,64,1024]{2,1,0:T(8,128)(2,1)}, bf16[2,512,256]{2,1,0:T(8,128)(2,1)}, bf16[2,4,2,512,256]{4,3,2,1,0:T(...) custom-call(bf16[2,512,1024]{2,1,0:T(8,128)(2,1)} %refs_6_.3, ...), custom_call_target="tpu_custom_call" | custom-call | flops 22000001024 | bytes 20000000 | tf_op jit(solution)/shard_map/front/pallas_call | solution.py:851
  135.3 115.2 %back.1 = (bf16[2,512,1024]{2,1,0:T(8,128)(2,1)}, f32[2,512,1024]{2,1,0:T(8,128)}, bf16[1024,256]{1,0:T(8,128)(2,1)}, f32[8,512]{1,0:T(8,128)}, bf16[2,128,512]{...) custom-call(bf16[352,512]{1,0:T(8,128)(2,1)} %get-tuple-element.52.r, ...), custom_call_target="tpu_custom_call" | custom-call | flops 30000001024 | bytes 10000000 | tf_op jit(solution)/shard_map/back/pallas_call | solution.py:1300
  250.6 9.5 %finish.1 = (f32[2,512,1024]{2,1,0:T(8,128)}, bf16[2,512,1024]{2,1,0:T(8,128)(2,1)}, f32[2,512,256]{2,1,0:T(8,128)}, f32[2,256,256]{2,1,0:T(8,128)}, f32[2,256,2...) custom-call(f32[2,512,1024]{2,1,0:T(8,128)} %get-tuple-element.69.re, ...), custom_call_target="tpu_custom_call" | custom-call | flops 1000000 | bytes 25000000 | tf_op jit(solution)/shard_map/finish/pallas_call | solution.py:1369

commit v2 on v1

--- a/solution.py
+++ b/solution.py
@@ -33,6 +33,8 @@
 
 
 class Sum:
+    lag = 2
+
     def __init__(self, place, part, inward, across, sems, done):
         self.pair = near(place)
         self.middle = 3 - place
@@ -84,9 +86,9 @@
             def _(i):
                 self.take_in(i)
 
-                @pl.when(i > 0)
+                @pl.when(i >= self.lag)
                 def _():
-                    self.finish(i - 1)
+                    self.finish(i - self.lag)
 
     def settled(self, first, count):
         @pl.when(self.outer)
@@ -101,7 +103,8 @@
     def close(self, count):
         @pl.when(self.inner)
         def _():
-            self.finish(count - 1)
+            for n in range(self.lag):
+                self.finish(count - self.lag + n)
 
             @pl.loop(0, count)
             def _(i):
@@ -886,7 +889,7 @@
     middle = dim // 2
     lines = seqs * per_seq
     count = 2 * lines - per_tile
-    head_start = per_seq + 2
+    head_start = per_seq + 3
     rest = 2 * per_seq - per_tile - head_start
     rest_start = head_start + per_seq
     own_start = (head_start, rest_start + rest)
@@ -1088,8 +1091,7 @@
         def _():
             ready(*names)
 
-    plan = [(1, m, line) for line, m in enumerate((0, 2, 3, 5, 7))] + [
-        (2, m, 9 + line) for line, m in enumerate((1, 3, 4, 6))]
+    plan = [(1, m, m) for m in range(7)] + [(2, m, 10 + line) for line, m in enumerate((0, 1, 3, 4, 6, 7))]
 
     @pl.loop(0, seqs + 1)
     def _(phase):
@@ -1100,6 +1102,8 @@
         def _():
             for wanted in range(seqs):
                 at_phase(phase, wanted + 1, [f"kv{wanted}"])
+            for wanted in range(1, seqs):
+                at_phase(phase, 1, [f"tok{wanted}", f"attn{wanted}"])
             dqt[...] = jnp.zeros_like(dqt)
 
             @pl.loop(0, 4)
@@ -1154,21 +1158,21 @@
         @pl.when(phase < seqs)
         def _():
             for wanted in range(seqs):
-                at_phase(phase, wanted, [
-                    f"{name}{wanted}" for name in ("tok", "attn", "cot", "mixed", "q", "ctx")])
+                names = ("tok", "attn") * (wanted == 0) + ("cot", "mixed", "q", "ctx")
+                at_phase(phase, wanted, [f"{name}{wanted}" for name in names])
             hidden_stage(phase)
             start_at(phase, "cot", "mixed")
 
             @pl.when(phase == 1)
             def _():
-                sums.steps(5, 1)
+                sums.steps(7, 1)
 
         @pl.when(phase > 0)
         def _():
             at_phase(phase, 1, ["wq", "wk", "wv", "rest"])
-            sums.steps(jnp.where(phase == 1, 6, 13), jnp.where(phase == 1, 1, 2))
+            sums.steps(jnp.where(phase == 1, 8, 16), 1)
             finalize(s)
-            sums.steps(jnp.where(phase == 1, 7, 15), 1)
+            sums.steps(jnp.where(phase == 1, 9, 17), 1)
 
         @pl.when(phase == seqs - 1)
         def _():
@@ -1181,9 +1185,8 @@
                 ends[0].fourth()
                 ready("quarter1")
                 ends[1].resume()
-            sums.steps(8, 1)
-
-    begun = 16
+
+    begun = 18
     fv_copy = pltpu.make_async_copy(proj.at[2], fv_hbm, fv_save)
     fv_copy.start()
     if split:
@@ -1217,22 +1220,22 @@
     sums.steps(begun + 2, 1)
     fold_q.second()
     fold_o.fourth()
-    sums.steps(begun + 3, 2)
+    sums.steps(begun + 3, 1)
     fold_k.third()
+    sums.steps(begun + 4, 1)
+    fold_v.third()
     sums.steps(begun + 5, 1)
-    fold_v.third()
-    sums.steps(begun + 6, 1)
     fold_q.third()
     fold_k.fourth()
+    sums.steps(begun + 6, 1)
+    fold_v.fourth()
     sums.steps(begun + 7, 1)
-    fold_v.fourth()
-    sums.steps(begun + 8, 1)
     fold_q.fourth()
     for fold in (fold_o, fold_k, fold_v) + tuple(ends[1:2]):
         fold.last()
     if split:
         ends[2].fourth()
-    sums.steps(begun + 9, count - begun - 9)
+    sums.steps(begun + 8, count - begun - 8)
     for fold in (fold_q,) + tuple(ends[2:]):
         fold.last()
     sums.settled(0, count)

time: 260 us -> 248 us (0.954)
  Pallas kernels: 259 us -> 247 us
    pallas_call x1, Pallas kernels: 115 us -> 105 us  [back(): pl.pallas_call(functools.partial(back_kernel, split), name='back', out_sh...]
where the time goes in v2:
time: 248 us
  Pallas kernels  247 us (100%)
    pallas_call x1, Pallas kernels, front(): pl.pallas_call(functools.partial(front_kernel, split), name='front', out_...  133 us
    pallas_call x1, Pallas kernels, back(): pl.pallas_call(functools.partial(back_kernel, split), name='back', out_sh...  105 us
    pallas_call x1, Pallas kernels, finish(): pl.pallas_call(functools.partial(finish_kernel, parts), name='finish', ou...  9.49 us

profile of v2, /device:TPU:0, one launch (start us, length us, event | category | flops | bytes accessed | tf_op | source)
XLA Modules:
  0.0 248.0 jit_solution(14705499096417306263)
XLA Ops:
  0.6 133.1 %front.1 = (bf16[20,64,1024]{2,1,0:T(8,128)(2,1)}, bf16[12,64,1024]{2,1,0:T(8,128)(2,1)}, bf16[2,512,256]{2,1,0:T(8,128)(2,1)}, bf16[2,4,2,512,256]{4,3,2,1,0:T(...) custom-call(bf16[2,512,1024]{2,1,0:T(8,128)(2,1)} %refs_6_.3, ...), custom_call_target="tpu_custom_call" | custom-call | flops 22000001024 | bytes 20000000 | tf_op jit(solution)/shard_map/front/pallas_call | solution.py:854
  133.7 104.5 %back.1 = (bf16[2,512,1024]{2,1,0:T(8,128)(2,1)}, f32[2,512,1024]{2,1,0:T(8,128)}, bf16[1024,256]{1,0:T(8,128)(2,1)}, f32[8,512]{1,0:T(8,128)}, bf16[2,128,512]{...) custom-call(bf16[352,512]{1,0:T(8,128)(2,1)} %get-tuple-element.52.r, ...), custom_call_target="tpu_custom_call" | custom-call | flops 30000001024 | bytes 10000000 | tf_op jit(solution)/shard_map/back/pallas_call | solution.py:1303
  238.3 9.5 %finish.1 = (f32[2,512,1024]{2,1,0:T(8,128)}, bf16[2,512,1024]{2,1,0:T(8,128)(2,1)}, f32[2,512,256]{2,1,0:T(8,128)}, f32[2,256,256]{2,1,0:T(8,128)}, f32[2,256,2...) custom-call(f32[2,512,1024]{2,1,0:T(8,128)} %get-tuple-element.69.re, ...), custom_call_target="tpu_custom_call" | custom-call | flops 1000000 | bytes 25000000 | tf_op jit(solution)/shard_map/finish/pallas_call | solution.py:1372

commit v3 on v2

--- a/solution.py
+++ b/solution.py
@@ -596,11 +596,11 @@
             vt[...] = jnp.transpose(kv[s, j, 1])
             key_pos = block_place(ring, j) * rows + lax.broadcasted_iota(jnp.int32, (rows, 1), 0)
             query_pos = ring * rows + lax.rem(lax.broadcasted_iota(jnp.int32, (1, 2 * rows), 1), rows)
-            seen = key_pos < jnp.maximum(query_pos + 1, prefix[s])
+            limit = jnp.maximum(query_pos + 1, prefix[s])
 
             @pl.loop(0, heads // 2)
             def _(h):
-                scores = jnp.where(seen, dot(kv[s, j, 0], qtm[s, h]), masked_score)
+                scores = jnp.where(key_pos < limit, dot(kv[s, j, 0], qtm[s, h]), masked_score)
                 old = maxes[h]
                 new = jnp.maximum(old, jnp.max(scores, axis=0, keepdims=True))
                 weights = jnp.exp(scores - new)
@@ -947,7 +947,7 @@
 
     def saving_token(i, n):
         s, own = chunk_at(n)
-        return pltpu.make_async_copy(hid.at[s, own], token_hbm.at[s, own], save.at[i])
+        return pltpu.make_async_copy(across.at[i], token_hbm.at[s, own], save.at[i])
 
     def add_gain(which, value):
         for piece in range(2):
@@ -974,8 +974,8 @@
             factor = lax.rsqrt(jnp.mean(values * values, axis=-1, keepdims=True) + epsilon)
             scaled = upstream * gain_one
             add_gain(0, jnp.sum(upstream * values * factor, axis=0, keepdims=True))
-            hid[s, own, :] += factor * scaled - values * factor**3 * jnp.mean(
-                scaled * values, axis=-1, keepdims=True)
+            across[i] = (hid[s, own, :] + factor * scaled - values * factor**3 * jnp.mean(
+                scaled * values, axis=-1, keepdims=True)).astype(bf16)
             saving_token(i, n).start()
 
     sums = Sum(place, part, inward, across, (send_one, recv_one, send_two, recv_two), done)
@@ -1031,14 +1031,14 @@
         kt[...] = jnp.transpose(kv[j, 0])
         key_pos = block_place(ring, j) * rows + lax.broadcasted_iota(jnp.int32, (rows, 1), 0)
         query_pos = ring * rows + lax.rem(lax.broadcasted_iota(jnp.int32, (1, 2 * rows), 1), rows)
-        seen = key_pos < jnp.maximum(query_pos + 1, prefix[s])
+        limit = jnp.maximum(query_pos + 1, prefix[s])
         dk[...] = jnp.zeros_like(dk)
         dv[...] = jnp.zeros_like(dv)
 
         @pl.loop(0, heads // 2)
         def _(h):
             scores = dot(kv[j, 0], qtm[h])
-            probs = jnp.where(seen, jnp.exp(scores - lse[s, pl.ds(h, 1), :]), 0.0)
+            probs = jnp.where(key_pos < limit, jnp.exp(scores - lse[s, pl.ds(h, 1), :]), 0.0)
             dprobs = dot(kv[j, 1], otm[h])
             dv[...] += dot(probs.astype(bf16), om[h])
             dscores = (probs * (dprobs - delta[h])).astype(bf16)
@@ -1304,7 +1304,7 @@
         functools.partial(back_kernel, split),
         name="back",
         out_shape=[
-            shape((seqs, rows, dim), bf16), shape((seqs, rows, dim), f32), shape((tokens, width), bf16),
+            shape((seqs, rows, dim), bf16), shape((seqs, rows, dim), bf16), shape((tokens, width), bf16),
             shape((8, dim // 2) if split else (2, 8, dim // 2), f32)] + fold_outs + ends_outs,
         in_specs=[anyw] * (len(quarters) + 12) + [vmem] * 4 + [pl.BlockSpec(memory_space=pltpu.SMEM)],
         out_specs=[anyw, anyw, anyw, vmem] + [anyw] * (4 + len(quarters)),
@@ -1363,7 +1363,7 @@
 
 
 def finish(arrays, types, gain_rows):
-    parts = [2 if x.size > 300000 else 1 for x in arrays]
+    parts = [x.shape[0] if x.size > 300000 else 1 for x in arrays]
     vmem = pl.BlockSpec(memory_space=pltpu.VMEM)
     anyw = pl.BlockSpec(memory_space=pl.ANY)
     dma = pltpu.SemaphoreType.DMA
@@ -1415,15 +1415,17 @@
         context.reshape(query.shape), log_total, cosine, sine, prefix)
     half_value_grad = half_value_grad.reshape(seqs, rows, width)
     if split:
-        arrays = (token_grad, block_out, half_value_grad, query_grad, key_grad, value_grad, out_grad, *ends)
+        cut = lambda x: x.reshape(8, -1, dim)
+        arrays = (cut(token_grad), cut(block_out), half_value_grad, query_grad, key_grad, value_grad, out_grad, *ends)
         (token_grad, block_out, half_value_grad, query_grad, key_grad, value_grad, out_grad, down_grad, gate_grad,
          up_grad, gain_one_grad, gain_two_grad) = finish(arrays, (f32, bf16) + (f32,) * 8, gain_grads)
+        token_grad, block_out = token_grad.reshape(tokens.shape), block_out.reshape(tokens.shape)
         over_rows = lambda grad: grad.reshape(-1, grad.shape[-1])
         over_columns = over_rows
         over_turned = lambda grad: over_rows(grad).T
         gain_one_grad, gain_two_grad = gain_one_grad[0], gain_two_grad[0]
     else:
-        half_value_grad = half_value_grad.astype(f32)
+        half_value_grad, token_grad = half_value_grad.astype(f32), token_grad.astype(f32)
         total = lambda grad, axis: lax.psum(
             lax.psum_scatter(grad, "fsdp", scatter_dimension=axis, tiled=True), "ctx").astype(f32)
         over_rows = lambda grad: total(jnp.swapaxes(grad, 0, 1).reshape(-1, grad.shape[-1]), 0)

time: 248 us -> 248 us (level)
  no operation moved by 1% of the time
where the time goes in v3:
time: 248 us
  Pallas kernels  247 us (100%)
    pallas_call x1, Pallas kernels, front(): pl.pallas_call(functools.partial(front_kernel, split), name='front', out_...  133 us
    pallas_call x1, Pallas kernels, back(): pl.pallas_call(functools.partial(back_kernel, split), name='back', out_sh...  105 us
    pallas_call x1, Pallas kernels, finish(): pl.pallas_call(functools.partial(finish_kernel, parts), name='finish', ou...  9.14 us

profile of v3, /device:TPU:0, one launch (start us, length us, event | category | flops | bytes accessed | tf_op | source)
XLA Modules:
  0.0 247.5 jit_solution(5839134763378046427)
XLA Ops:
  0.6 133.0 %front.1 = (bf16[20,64,1024]{2,1,0:T(8,128)(2,1)}, bf16[12,64,1024]{2,1,0:T(8,128)(2,1)}, bf16[2,512,256]{2,1,0:T(8,128)(2,1)}, bf16[2,4,2,512,256]{4,3,2,1,0:T(...) custom-call(bf16[2,512,1024]{2,1,0:T(8,128)(2,1)} %refs_6_.3, ...), custom_call_target="tpu_custom_call" | custom-call | flops 22000001024 | bytes 20000000 | tf_op jit(solution)/shard_map/front/pallas_call | solution.py:854
  133.7 104.5 %back.1 = (bf16[2,512,1024]{2,1,0:T(8,128)(2,1)}, bf16[2,512,1024]{2,1,0:T(8,128)(2,1)}, bf16[1024,256]{1,0:T(8,128)(2,1)}, f32[8,512]{1,0:T(8,128)}, bf16[2,128...) custom-call(bf16[352,512]{1,0:T(8,128)(2,1)} %get-tuple-element.52.r, ...), custom_call_target="tpu_custom_call" | custom-call | flops 30000001024 | bytes 10000000 | tf_op jit(solution)/shard_map/back/pallas_call | solution.py:1303
  238.2 9.1 %finish.1 = (f32[8,128,1024]{2,1,0:T(8,128)}, bf16[8,128,1024]{2,1,0:T(8,128)(2,1)}, f32[2,512,256]{2,1,0:T(8,128)}, f32[2,256,256]{2,1,0:T(8,128)}, f32[2,256,2...) custom-call(bf16[8,128,1024]{2,1,0:T(8,128)(2,1)} %bitcast.24, ...), custom_call_target="tpu_custom_call" | custom-call | flops 1000000 | bytes 25000000 | tf_op jit(solution)/shard_map/finish/pallas_call | solution.py:1372

commit v4 on v3

--- a/solution.py
+++ b/solution.py
@@ -1035,8 +1035,7 @@
         dk[...] = jnp.zeros_like(dk)
         dv[...] = jnp.zeros_like(dv)
 
-        @pl.loop(0, heads // 2)
-        def _(h):
+        def per_pair(h):
             scores = dot(kv[j, 0], qtm[h])
             probs = jnp.where(key_pos < limit, jnp.exp(scores - lse[s, pl.ds(h, 1), :]), 0.0)
             dprobs = dot(kv[j, 1], otm[h])
@@ -1047,6 +1046,9 @@
                 of_head = rows_at((2 * h + n) * HEAD_DIM, HEAD_DIM)
                 dqt[of_head, :] += dot(kt[of_head, :], dscores[:, n * rows : (n + 1) * rows])
             tick(h)
+
+        for h in range(heads // 2):
+            per_pair(h)
 
     def finalize(s):
         near_to_mate(s).wait_recv()

time: 248 us -> 248 us (level)
  no operation moved by 1% of the time
where the time goes in v4:
time: 248 us
  Pallas kernels  247 us (100%)
    pallas_call x1, Pallas kernels, front(): pl.pallas_call(functools.partial(front_kernel, split), name='front', out_...  133 us
    pallas_call x1, Pallas kernels, back(): pl.pallas_call(functools.partial(back_kernel, split), name='back', out_sh...  105 us
    pallas_call x1, Pallas kernels, finish(): pl.pallas_call(functools.partial(finish_kernel, parts), name='finish', ou...  9.14 us

profile of v4, /device:TPU:0, one launch (start us, length us, event | category | flops | bytes accessed | tf_op | source)
XLA Modules:
  0.0 247.5 jit_solution(13172464947727393766)
XLA Ops:
  0.6 133.0 %front.1 = (bf16[20,64,1024]{2,1,0:T(8,128)(2,1)}, bf16[12,64,1024]{2,1,0:T(8,128)(2,1)}, bf16[2,512,256]{2,1,0:T(8,128)(2,1)}, bf16[2,4,2,512,256]{4,3,2,1,0:T(...) custom-call(bf16[2,512,1024]{2,1,0:T(8,128)(2,1)} %refs_6_.3, ...), custom_call_target="tpu_custom_call" | custom-call | flops 22000001024 | bytes 20000000 | tf_op jit(solution)/shard_map/front/pallas_call | solution.py:854
  133.7 104.5 %back.1 = (bf16[2,512,1024]{2,1,0:T(8,128)(2,1)}, bf16[2,512,1024]{2,1,0:T(8,128)(2,1)}, bf16[1024,256]{1,0:T(8,128)(2,1)}, f32[8,512]{1,0:T(8,128)}, bf16[2,128...) custom-call(bf16[352,512]{1,0:T(8,128)(2,1)} %get-tuple-element.52.r, ...), custom_call_target="tpu_custom_call" | custom-call | flops 30000001024 | bytes 10000000 | tf_op jit(solution)/shard_map/back/pallas_call | solution.py:1305
  238.2 9.1 %finish.1 = (f32[8,128,1024]{2,1,0:T(8,128)}, bf16[8,128,1024]{2,1,0:T(8,128)(2,1)}, f32[2,512,256]{2,1,0:T(8,128)}, f32[2,256,256]{2,1,0:T(8,128)}, f32[2,256,2...) custom-call(bf16[8,128,1024]{2,1,0:T(8,128)(2,1)} %bitcast.24, ...), custom_call_target="tpu_custom_call" | custom-call | flops 1000000 | bytes 25000000 | tf_op jit(solution)/shard_map/finish/pallas_call | solution.py:1374
